TPU v7x, 32 devices: a whole 2x2x4 slice. The times are simulated.
32 devices in a mesh: frm: 4 (over z), vox: 8 (over y, x, core).
Axes of the slice: x: 2, y: 2, z: 4, core: 2. Of those that a mesh axis runs over, the one named last changes fastest.
Arguments:
- movie_matrix: bfloat16 [8192, 16384], P('frm', 'vox'), may hold values from -8 to 8
- voxel_probe: bfloat16 [16384, 64], P('vox'), may hold values from -0.046875 to 0.046875
- frame_probe: bfloat16 [8192, 64], P('frm'), may hold values from -0.0625 to 0.0625
Outputs:
- lowrank: bfloat16 [8192, 16384], P('frm', 'vox')
- sparse: bfloat16 [8192, 16384], P('frm', 'vox')
All inputs are finite; a program needn't handle non-finite values.
Results may differ from a plain program's by a relative error of at most 0.04.
Values may be sent and summed in bfloat16 or wider, within the bound.
No kernel may reach another device: no remote copies, remote signals or barrier semaphores. Data moves between devices by JAX's collectives and lax.ppermute only.
A program may use at most 128 MiB of HBM per device.

v0:
```python
import functools

import jax
import jax.numpy as jnp
from jax import lax
from jax.experimental import pallas as pl
from jax.experimental.pallas import tpu as pltpu
from jax.sharding import PartitionSpec as P

ITERS = 2
cutoff = 1.0
ridge_scale = 0.1


F32 = jnp.float32
BF16 = jnp.bfloat16
LANES = 128


def dot(a, b, contract=((1,), (0,))):
    return lax.dot_general(a, b, (contract, ((), ())), preferred_element_type=F32)


def split2(x):
    high = x.astype(BF16)
    return high, (x - high.astype(F32)).astype(BF16)


def pack_core(core):
    high, low = split2(core)
    return jnp.concatenate([high, low], axis=1)


def unpack_core(packed):
    rank = packed.shape[0]
    wide = packed.astype(F32)
    return wide[:, :rank] + wide[:, rank:]


def finish_sketch(where_ref, y1_scr, y2_scr, vpt_ref, own_ref, send_ref, y2_refs):
    rank, frames = y1_scr.shape
    half = frames // 2
    peers = len(y2_refs)
    share = y2_scr.shape[1] // peers
    y2 = y2_scr[...]
    high, rest = split2(y2)
    low = (y2 - high.astype(F32) - rest.astype(F32)).astype(BF16)
    vp = vpt_ref[...]
    core = sum(dot(part, vp, ((1,), (1,))) for part in (high, rest, low))
    side = where_ref[0]
    row = where_ref[1]
    own_ref[:, :half] = y1_scr[:, pl.ds(pl.multiple_of(side * half, LANES), half)]
    own_ref[:, half : half + 2 * rank] = jnp.concatenate([core, jnp.zeros_like(core)], axis=1)
    other = y1_scr[:, pl.ds(pl.multiple_of((1 - side) * half, LANES), half)]
    send_ref[:, :half] = other.astype(BF16)
    send_ref[:, half : half + 2 * rank] = pack_core(core)
    for k in range(peers):
        slot = jnp.bitwise_xor(row, k)
        part = y2_scr[:, pl.ds(pl.multiple_of(slot * share, LANES), share)]
        y2_refs[k][...] = part.astype(y2_refs[k].dtype)


def first_kernel(where_ref, movie_ref, vpt_ref, fpt_ref, own_ref, send_ref, *rest):
    *y2_refs, y1_scr, y2_scr = rest
    step = pl.program_id(0)
    rows = movie_ref.shape[0]

    @pl.when(step == 0)
    def _():
        y2_scr[...] = jnp.zeros_like(y2_scr)

    cur = movie_ref[...]
    y2_scr[...] += dot(fpt_ref[...], cur)
    y1_scr[:, pl.ds(pl.multiple_of(step * rows, rows), rows)] = dot(vpt_ref[...], cur, ((1,), (1,)))

    @pl.when(step == pl.num_programs(0) - 1)
    def _():
        finish_sketch(where_ref, y1_scr, y2_scr, vpt_ref, own_ref, send_ref, y2_refs)


def pair_kernel(own_ref, got_ref, msg_ref):
    rank, width = own_ref.shape
    half = width - 2 * rank
    msg_ref[:, :half] = (own_ref[:, :half] + got_ref[:, :half].astype(F32)).astype(BF16)
    core = own_ref[:, half:][:, :rank] + unpack_core(got_ref[:, half:])
    msg_ref[:, half:] = pack_core(core)


def plane_kernel(*refs):
    *plane_refs, half_ref, core_ref = refs
    half = half_ref.shape[1]
    total = plane_refs[0][:, :half].astype(F32)
    core = unpack_core(plane_refs[0][:, half:])
    for ref in plane_refs[1:]:
        total += ref[:, :half].astype(F32)
        core += unpack_core(ref[:, half:])
    core_ref[...] = pack_core(core)
    half_ref[...] = total.astype(BF16)


def add_kernel(*refs):
    *parts, sum_ref = refs
    total = parts[0][...]
    for ref in parts[1:]:
        total += ref[...].astype(F32)
    sum_ref[...] = total.astype(BF16)


def solve_mixer(core):
    rank = core.shape[0]
    gram = lax.dot_general(
        core, core, (((0,), (0,)), ((), ())), precision=lax.Precision.HIGHEST, preferred_element_type=F32
    )
    r = lax.broadcasted_iota(jnp.int32, (rank, rank), 0)
    c = lax.broadcasted_iota(jnp.int32, (rank, rank), 1)
    eye = (r == c).astype(F32)
    shift = ridge_scale * (jnp.sum(gram * eye) / rank + 1e-06)
    table = jnp.concatenate([gram + shift * eye, core.T], axis=1)
    width = table.shape[1]
    tall = 8
    tile = (tall, width)
    line = lax.broadcasted_iota(jnp.int32, tile, 0)
    tiles = [table[i : i + tall, :] for i in range(0, rank, tall)]
    for k in range(0, rank, 4):
        own, i = k // tall, k % tall
        cols = [[jnp.broadcast_to(t[:, k + j : k + j + 1], tile) for t in tiles] for j in range(4)]
        row = lambda t, j: jnp.broadcast_to(t[i + j : i + j + 1, :], tile)
        at = lambda m, j: row(cols[j][own], m)
        r0, r1, r2, r3 = [row(tiles[own], j) for j in range(4)]
        a, b, d = at(0, 0), at(1, 0), at(1, 1)
        e0, e1, f0, f1 = at(2, 0), at(2, 1), at(3, 0), at(3, 1)
        inv = 1.0 / (a * d - b * b)
        u0, u1 = (d * e0 - b * e1) * inv, (a * e1 - b * e0) * inv
        v0, v1 = (d * f0 - b * f1) * inv, (a * f1 - b * f0) * inv
        p = at(2, 2) - (e0 * u0 + e1 * u1)
        q = at(3, 2) - (e0 * v0 + e1 * v1)
        t = at(3, 3) - (f0 * v0 + f1 * v1)
        inv_late = 1.0 / (p * t - q * q)
        n0, n1 = (r0 * d - r1 * b) * inv, (r1 * a - r0 * b) * inv
        s2, s3 = r2 - (e0 * n0 + e1 * n1), r3 - (f0 * n0 + f1 * n1)
        n2, n3 = (s2 * t - s3 * q) * inv_late, (s3 * p - s2 * q) * inv_late
        n0, n1 = n0 - (u0 * n2 + v0 * n3), n1 - (u1 * n2 + v1 * n3)
        for j in range(4):
            cols[j][own] = cols[j][own] - (line == i + j).astype(F32)
        tiles = [
            x - ((c0 * n0 + c1 * n1) + (c2 * n2 + c3 * n3)) for x, c0, c1, c2, c3 in zip(tiles, *cols)
        ]
    return jnp.concatenate(tiles, axis=0)[:, rank:]


def solve_kernel(where_ref, own_half_ref, got_half_ref, *rest):
    *core_refs, left_ref = rest
    half = own_half_ref.shape[1]
    core = unpack_core(core_refs[0][...])
    for ref in core_refs[1:]:
        core += unpack_core(ref[...])
    high, low = split2(solve_mixer(core))
    side = where_ref[0]
    for k, ref in enumerate((own_half_ref, got_half_ref)):
        y1 = ref[...]
        left = dot(y1, high, ((0,), (0,))) + dot(y1, low, ((0,), (0,)))
        slot = jnp.bitwise_xor(side, k)
        left_ref[pl.ds(pl.multiple_of(slot * half, half), half), :] = left.astype(BF16)


def join_right(where_ref, right_refs, right_scr):
    share = right_refs[0].shape[1]
    for k, ref in enumerate(right_refs):
        slot = jnp.bitwise_xor(where_ref[1], k)
        right_scr[:, pl.ds(pl.multiple_of(slot * share, LANES), share)] = ref[...]


def middle_kernel(n_row, chunk, where_ref, movie_ref, vpt_ref, fpt_ref, left_ref, *rest):
    right_refs = rest[:n_row]
    own_ref, send_ref = rest[n_row : 2 + n_row]
    *y2_refs, right_scr, cur_scr, y1_scr, y2_scr = rest[2 + n_row :]
    step = pl.program_id(0)
    rows, voxels = cur_scr.shape

    @pl.when(step == 0)
    def _():
        join_right(where_ref, right_refs, right_scr)
        y2_scr[...] = jnp.zeros_like(y2_scr)

    span = pl.ds(pl.multiple_of(step * rows, rows), rows)
    left = left_ref[span, :]
    fpt = fpt_ref[...]
    cols = [slice(j, j + chunk) for j in range(0, voxels, chunk)]
    bound = jnp.asarray(cutoff, BF16)

    def sketch(c, y1):
        cur = cur_scr[:, c]
        y2_scr[:, c] += dot(fpt, cur)
        part = dot(vpt_ref[:, c], cur, ((1,), (1,)))
        return part if y1 is None else y1 + part

    y1 = None
    ahead = dot(left, right_scr[:, cols[0]])
    for j, c in enumerate(cols):
        low = ahead.astype(BF16)
        if j + 1 < len(cols):
            ahead = dot(left, right_scr[:, cols[j + 1]])
        cur_scr[:, c] = low + jnp.clip(movie_ref[span, c] - low, -bound, bound)
        if j > 0:
            y1 = sketch(cols[j - 1], y1)
    y1_scr[:, span] = sketch(cols[-1], y1)

    @pl.when(step == pl.num_programs(0) - 1)
    def _():
        finish_sketch(where_ref, y1_scr, y2_scr, vpt_ref, own_ref, send_ref, y2_refs)


def last_kernel(n_row, chunk, where_ref, movie_ref, left_ref, *rest):
    right_refs = rest[:n_row]
    low_ref, sparse_ref, right_scr = rest[n_row:]
    step = pl.program_id(0)
    rows, voxels = low_ref.shape

    @pl.when(step == 0)
    def _():
        join_right(where_ref, right_refs, right_scr)

    span = pl.ds(pl.multiple_of(step * rows, rows), rows)
    left = left_ref[span, :]
    cols = [slice(j, j + chunk) for j in range(0, voxels, chunk)]
    ahead = dot(left, right_scr[:, cols[0]])
    for j, c in enumerate(cols):
        low = ahead
        if j + 1 < len(cols):
            ahead = dot(left, right_scr[:, cols[j + 1]])
        low_ref[:, c] = low.astype(BF16)
        gap = movie_ref[span, c].astype(F32) - low
        sparse_ref[:, c] = (gap - jnp.clip(gap, -cutoff, cutoff)).astype(BF16)


def block_rows(rows, width):
    return pl.BlockSpec((rows, width), lambda i, *_: (i, 0))


def block_cols(rank, rows):
    return pl.BlockSpec((rank, rows), lambda i, *_: (0, i))


def size_of(arrays):
    return sum(a.size * a.dtype.itemsize for a in arrays)


def vmem_call(kernel, outs, args, flops=1e6, where=None):
    resident = pl.BlockSpec(memory_space=pltpu.VMEM)
    return pl.pallas_call(
        kernel,
        out_shape=outs,
        in_specs=([] if where is None else [pl.BlockSpec(memory_space=pltpu.SMEM)]) + [resident] * len(args),
        out_specs=[resident] * len(outs),
        compiler_params=pltpu.CompilerParams(vmem_limit_bytes=8 * 1024 * 1024),
        cost_estimate=pl.CostEstimate(flops=int(flops), bytes_accessed=size_of([*args, *outs]), transcendentals=0),
    )(*([] if where is None else [where]), *args)


def exchange(x, axis, k):
    size = lax.axis_size(axis)
    return lax.ppermute(x, axis, [(i, i ^ k) for i in range(size)])


def on_device(movie, voxel_probe, frame_probe):
    frames, voxels = movie.shape
    rank = voxel_probe.shape[1]
    n_vox, n_row = lax.axis_size("vox"), lax.axis_size("frm")
    half, share = frames // 2, voxels // n_row
    width = half + 2 * rank
    rows = min(512, frames)
    last_rows = min(256, frames)
    chunk = min(256, voxels)
    where = jnp.stack([lax.axis_index("vox") % 2, lax.axis_index("frm")]).astype(jnp.int32)
    vpt, fpt = voxel_probe.T, frame_probe.T

    resident = pl.BlockSpec(memory_space=pltpu.VMEM)
    sketch_shapes = [
        jax.ShapeDtypeStruct((rank, width), F32),
        jax.ShapeDtypeStruct((rank, width), BF16),
        jax.ShapeDtypeStruct((rank, share), F32),
    ] + [jax.ShapeDtypeStruct((rank, share), BF16)] * (n_row - 1)
    sketch_specs = [resident] * len(sketch_shapes)
    sums = [pltpu.VMEM((rank, frames), F32), pltpu.VMEM((rank, voxels), F32)]
    right = pltpu.VMEM((rank, voxels), BF16)
    probe_specs = [resident, block_cols(rank, rows)]
    side_specs = [resident] * (1 + n_row)

    def run(kernel, steps, in_specs, out_specs, out_shape, scratch, passes, args, limit=20 * 1024 * 1024):
        return pl.pallas_call(
            kernel,
            grid_spec=pltpu.PrefetchScalarGridSpec(
                num_scalar_prefetch=1,
                grid=(steps,),
                in_specs=in_specs,
                out_specs=out_specs,
                scratch_shapes=scratch,
            ),
            out_shape=out_shape,
            compiler_params=pltpu.CompilerParams(
                dimension_semantics=("arbitrary",), vmem_limit_bytes=limit
            ),
            cost_estimate=pl.CostEstimate(
                flops=2 * passes * frames * voxels * rank, bytes_accessed=2 * frames * voxels, transcendentals=0
            ),
        )(where, *args)

    def share_sketch(own, send, *y2_parts):
        got = exchange(send, "vox", 1)
        (msg,) = vmem_call(pair_kernel, [jax.ShapeDtypeStruct((rank, width), BF16)], [own, got])
        plane = [msg] + [exchange(msg, "vox", 2 * k) for k in range(1, n_vox // 2)]
        parts = [y2_parts[0]] + [exchange(y2_parts[k], "frm", k) for k in range(1, n_row)]
        own_half, core = vmem_call(
            plane_kernel,
            [jax.ShapeDtypeStruct((rank, half), BF16), jax.ShapeDtypeStruct((rank, 2 * rank), BF16)],
            plane,
        )
        cores = [core] + [exchange(core, "frm", k) for k in range(1, n_row)]
        got_half = exchange(own_half, "vox", 1)
        (mine,) = vmem_call(add_kernel, [jax.ShapeDtypeStruct((rank, share), BF16)], parts)
        rights = [mine] + [exchange(mine, "frm", k) for k in range(1, n_row)]
        (left,) = vmem_call(
            solve_kernel,
            [jax.ShapeDtypeStruct((frames, rank), BF16)],
            [own_half, got_half, *cores],
            flops=5e9,
            where=where,
        )
        return [left, *rights]

    sketch = run(
        first_kernel,
        frames // rows,
        [block_rows(rows, voxels), pl.BlockSpec((rank, voxels), lambda i, *_: (0, 0)), block_cols(rank, rows)],
        sketch_specs,
        sketch_shapes,
        sums,
        2,
        tuple(pltpu.with_memory_space_constraint(x, pltpu.HBM) for x in (movie, vpt, fpt)),
        limit=44 * 1024 * 1024,
    )
    sides = share_sketch(*sketch)
    for _ in range(1, ITERS):
        sketch = run(
            functools.partial(middle_kernel, n_row, chunk),
            frames // rows,
            [resident] + probe_specs + side_specs,
            sketch_specs,
            sketch_shapes,
            [right, pltpu.VMEM((rows, voxels), BF16)] + sums,
            3,
            (movie, vpt, fpt, *sides),
        )
        sides = share_sketch(*sketch)
    out = jax.ShapeDtypeStruct((frames, voxels), BF16)
    return tuple(
        run(
            functools.partial(last_kernel, n_row, chunk),
            frames // last_rows,
            [resident] + side_specs,
            [block_rows(last_rows, voxels)] * 2,
            [out, out],
            [right],
            1,
            (movie, *sides),
        )
    )


def solution(mesh):
    return jax.shard_map(
        on_device,
        mesh=mesh,
        in_specs=(P("frm", "vox"), P("vox", None), P("frm", None)),
        out_specs=(P("frm", "vox"), P("frm", "vox")),
        check_vma=False,
    )
```

profile of v0, /device:TPU:0, one launch (start us, length us, event | category | flops | bytes accessed | tf_op | source)
XLA Modules:
  0.0 89.0 jit_solution(5947712737881643248)
XLA Ops:
  0.7 8.4 %shard_map.50 = (f32[64,1152]{1,0:T(8,128)S(1)}, bf16[64,1152]{1,0:T(8,128)(2,1)S(1)}, f32[64,512]{1,0:T(8,128)S(1)}, bf16[64,512]{1,0:T(8,128)(2,1)S(1)}, bf16[...) custom-call(s32[2]{0:T(128)S(1)} %pad_add_fusion.where_ref, bf16[2048,2048]{1,0:T(8,128)(2,1)} %movie_ref.5, ...), custom_call_target="tpu_custom_call" | custom-call | flops 1073741824 | bytes 8388608 | tf_op jit(solution)/shard_map/pallas_call | solution.py:290
  9.1 0.6 collective-permute-start
  9.6 1.0 %collective-permute-done.got_ref = bf16[64,1152]{1,0:T(8,128)(2,1)S(1)} collective-permute-done((bf16[64,1152]{1,0:T(8,128)(2,1)S(1)}, bf16[64,1152]{1,0:T(8,128)(2,1)S(1)}, u32[]{:S(2)}, u32[]{:S(2)}) %collective-permute-start) | collective-permute-done | bytes 147488 | tf_op jit(solution)/shard_map/ppermute | solution.py:262
  10.8 3.8 %collective-permute-start.3 = (bf16[64,1152]{1,0:T(8,128)(2,1)S(1)}, bf16[64,1152]{1,0:T(8,128)(2,1)S(1)}, u32[]{:S(2)}, u32[]{:S(2)}) collective-permute-start(bf16[64,1152]{1,0:T(8,128)(2,1)S(1)} %shard_map.51.refs_0_), channel_id=1, source_target_pairs={{0,6},{1,7},{2,4},{3,5},{4,2},{5,3},{6,0},{7,1},{8,14},{9,15},{10,... | collective-permute-start | bytes 442376 | tf_op jit(solution)/shard_map/ppermute | solution.py:262
  14.6 0.5 collective-permute-start.2
  15.3 4.0 %collective-permute-done.3.refs_3_ = bf16[64,1152]{1,0:T(8,128)(2,1)S(1)} collective-permute-done((bf16[64,1152]{1,0:T(8,128)(2,1)S(1)}, bf16[64,1152]{1,0:T(8,128)(2,1)S(1)}, u32[]{:S(2)}, u32[]{:S(2)}) %collective-permute-start.3) | collective-permute-done | bytes 147488 | tf_op jit(solution)/shard_map/ppermute | solution.py:262
  19.3 2.6 %collective-permute-done.2.refs_2_ = bf16[64,1152]{1,0:T(8,128)(2,1)S(1)} collective-permute-done((bf16[64,1152]{1,0:T(8,128)(2,1)S(1)}, bf16[64,1152]{1,0:T(8,128)(2,1)S(1)}, u32[]{:S(2)}, u32[]{:S(2)}) %collective-permute-start.2) | collective-permute-done | bytes 147488 | tf_op jit(solution)/shard_map/ppermute | solution.py:262
  22.5 1.6 %collective-permute-start.8 = (bf16[64,512]{1,0:T(8,128)(2,1)S(1)}, bf16[64,512]{1,0:T(8,128)(2,1)S(1)}, u32[]{:S(2)}, u32[]{:S(2)}) collective-permute-start(bf16[64,512]{1,0:T(8,128)(2,1)S(1)} %get-tuple-element.23), channel_id=1, source_target_pairs={{0,8},{8,0},{16,24},{24,16},{1,9},{9,1},{17,25},{25,17},{2,10},{10... | collective-permute-start | bytes 196616 | tf_op jit(solution)/shard_map/ppermute | solution.py:262
  24.1 2.6 %collective-permute-start.9 = (bf16[64,512]{1,0:T(8,128)(2,1)S(1)}, bf16[64,512]{1,0:T(8,128)(2,1)S(1)}, u32[]{:S(2)}, u32[]{:S(2)}) collective-permute-start(bf16[64,512]{1,0:T(8,128)(2,1)S(1)} %get-tuple-element.24), channel_id=1, source_target_pairs={{0,16},{8,24},{16,0},{24,8},{1,17},{9,25},{17,1},{25,9},{2,18},{10... | collective-permute-start | bytes 196616 | tf_op jit(solution)/shard_map/ppermute | solution.py:262
  26.9 3.6 %collective-permute-start.7 = (bf16[64,128]{1,0:T(8,128)(2,1)S(1)}, bf16[64,128]{1,0:T(8,128)(2,1)S(1)}, u32[]{:S(2)}, u32[]{:S(2)}) collective-permute-start(bf16[64,128]{1,0:T(8,128)(2,1)S(1)} %get-tuple-element.21.rest_0_), channel_id=1, source_target_pairs={{0,24},{8,16},{16,8},{24,0},{1,25},{9,17},{17,9},{25,1},{2,26},{10... | collective-permute-start | bytes 49160 | tf_op jit(solution)/shard_map/ppermute | solution.py:262
  30.5 2.5 %collective-permute-done.9.refs_2_ = bf16[64,512]{1,0:T(8,128)(2,1)S(1)} collective-permute-done((bf16[64,512]{1,0:T(8,128)(2,1)S(1)}, bf16[64,512]{1,0:T(8,128)(2,1)S(1)}, u32[]{:S(2)}, u32[]{:S(2)}) %collective-permute-start.9) | collective-permute-done | bytes 65568 | tf_op jit(solution)/shard_map/ppermute | solution.py:262
  33.2 2.6 %collective-permute-start.13 = (bf16[64,512]{1,0:T(8,128)(2,1)S(1)}, bf16[64,512]{1,0:T(8,128)(2,1)S(1)}, u32[]{:S(2)}, u32[]{:S(2)}) collective-permute-start(bf16[64,512]{1,0:T(8,128)(2,1)S(1)} %shard_map.54.rest_0_), channel_id=1, source_target_pairs={{0,24},{8,16},{16,8},{24,0},{1,25},{9,17},{17,9},{25,1},{2,26},{10... | collective-permute-start | bytes 196616 | tf_op jit(solution)/shard_map/ppermute | solution.py:262
  35.8 0.9 %collective-permute-start.12 = (bf16[64,512]{1,0:T(8,128)(2,1)S(1)}, bf16[64,512]{1,0:T(8,128)(2,1)S(1)}, u32[]{:S(2)}, u32[]{:S(2)}) collective-permute-start(bf16[64,512]{1,0:T(8,128)(2,1)S(1)} %shard_map.54.rest_0_), channel_id=1, source_target_pairs={{0,16},{8,24},{16,0},{24,8},{1,17},{9,25},{17,1},{25,9},{2,18},{10... | collective-permute-start | bytes 196616 | tf_op jit(solution)/shard_map/ppermute | solution.py:262
  36.7 0.9 %collective-permute-start.11 = (bf16[64,512]{1,0:T(8,128)(2,1)S(1)}, bf16[64,512]{1,0:T(8,128)(2,1)S(1)}, u32[]{:S(2)}, u32[]{:S(2)}) collective-permute-start(bf16[64,512]{1,0:T(8,128)(2,1)S(1)} %shard_map.54.rest_0_), channel_id=1, source_target_pairs={{0,8},{8,0},{16,24},{24,16},{1,9},{9,1},{17,25},{25,17},{2,10},{10... | collective-permute-start | bytes 196616 | tf_op jit(solution)/shard_map/ppermute | solution.py:262
  37.6 4.5 %shard_map.53.left_ref = bf16[2048,64]{1,0:T(8,128)(2,1)S(1)} custom-call(s32[2]{0:T(128)S(1)} %pad_add_fusion.where_ref, bf16[64,1024]{1,0:T(8,128)(2,1)S(1)} %get-tuple-element.20.own_half_ref, bf16[64,1024]{1,0:T(8,128)(2,1)S(1)} %collective-permute-done.4.got_half_ref, bf16[64,128]{1,0:T(8,128)(2,1)S(1)} %get-tuple-element.21.rest_0_, ...), custom_call_target="tpu_custom_call" | custom-call | flops 5000000000 | bytes 589824 | tf_op jit(solution)/shard_map/pallas_call | solution.py:250
  42.2 7.4 %shard_map.55 = (f32[64,1152]{1,0:T(8,128)S(1)}, bf16[64,1152]{1,0:T(8,128)(2,1)S(1)}, f32[64,512]{1,0:T(8,128)S(1)}, bf16[64,512]{1,0:T(8,128)(2,1)S(1)}, bf16[...) custom-call(s32[2]{0:T(128)S(1)} %pad_add_fusion.where_ref, bf16[2048,2048]{1,0:T(8,128)(2,1)S(1)} %bitcast.5, ...), custom_call_target="tpu_custom_call" | custom-call | flops 1610612736 | bytes 8388608 | tf_op jit(solution)/shard_map/pallas_call | solution.py:290
  49.7 1.4 %collective-permute-done.14.got_ref = bf16[64,1152]{1,0:T(8,128)(2,1)S(1)} collective-permute-done((bf16[64,1152]{1,0:T(8,128)(2,1)S(1)}, bf16[64,1152]{1,0:T(8,128)(2,1)S(1)}, u32[]{:S(2)}, u32[]{:S(2)}) %collective-permute-start.14) | collective-permute-done | bytes 147488 | tf_op jit(solution)/shard_map/ppermute | solution.py:262
  51.3 1.6 %collective-permute-start.17 = (bf16[64,1152]{1,0:T(8,128)(2,1)S(1)}, bf16[64,1152]{1,0:T(8,128)(2,1)S(1)}, u32[]{:S(2)}, u32[]{:S(2)}) collective-permute-start(bf16[64,1152]{1,0:T(8,128)(2,1)S(1)} %shard_map.56.refs_0_), channel_id=1, source_target_pairs={{0,6},{1,7},{2,4},{3,5},{4,2},{5,3},{6,0},{7,1},{8,14},{9,15},{10,... | collective-permute-start | bytes 442376 | tf_op jit(solution)/shard_map/ppermute | solution.py:262
  52.9 1.3 %collective-permute-start.16 = (bf16[64,1152]{1,0:T(8,128)(2,1)S(1)}, bf16[64,1152]{1,0:T(8,128)(2,1)S(1)}, u32[]{:S(2)}, u32[]{:S(2)}) collective-permute-start(bf16[64,1152]{1,0:T(8,128)(2,1)S(1)} %shard_map.56.refs_0_), channel_id=1, source_target_pairs={{0,4},{1,5},{2,6},{3,7},{4,0},{5,1},{6,2},{7,3},{8,12},{9,13},{10,... | collective-permute-start | bytes 442376 | tf_op jit(solution)/shard_map/ppermute | solution.py:262
  54.2 0.5 collective-permute-start.15
  54.8 4.2 %collective-permute-done.17.refs_3_ = bf16[64,1152]{1,0:T(8,128)(2,1)S(1)} collective-permute-done((bf16[64,1152]{1,0:T(8,128)(2,1)S(1)}, bf16[64,1152]{1,0:T(8,128)(2,1)S(1)}, u32[]{:S(2)}, u32[]{:S(2)}) %collective-permute-start.17) | collective-permute-done | bytes 147488 | tf_op jit(solution)/shard_map/ppermute | solution.py:262
  58.9 2.3 %collective-permute-done.16.refs_2_ = bf16[64,1152]{1,0:T(8,128)(2,1)S(1)} collective-permute-done((bf16[64,1152]{1,0:T(8,128)(2,1)S(1)}, bf16[64,1152]{1,0:T(8,128)(2,1)S(1)}, u32[]{:S(2)}, u32[]{:S(2)}) %collective-permute-start.16) | collective-permute-done | bytes 147488 | tf_op jit(solution)/shard_map/ppermute | solution.py:262
  61.5 1.2 %collective-permute-start.22 = (bf16[64,512]{1,0:T(8,128)(2,1)S(1)}, bf16[64,512]{1,0:T(8,128)(2,1)S(1)}, u32[]{:S(2)}, u32[]{:S(2)}) collective-permute-start(bf16[64,512]{1,0:T(8,128)(2,1)S(1)} %get-tuple-element.31), channel_id=1, source_target_pairs={{0,8},{8,0},{16,24},{24,16},{1,9},{9,1},{17,25},{25,17},{2,10},{10... | collective-permute-start | bytes 196616 | tf_op jit(solution)/shard_map/ppermute | solution.py:262
  62.7 2.0 %collective-permute-start.23 = (bf16[64,512]{1,0:T(8,128)(2,1)S(1)}, bf16[64,512]{1,0:T(8,128)(2,1)S(1)}, u32[]{:S(2)}, u32[]{:S(2)}) collective-permute-start(bf16[64,512]{1,0:T(8,128)(2,1)S(1)} %get-tuple-element.32), channel_id=1, source_target_pairs={{0,16},{8,24},{16,0},{24,8},{1,17},{9,25},{17,1},{25,9},{2,18},{10... | collective-permute-start | bytes 196616 | tf_op jit(solution)/shard_map/ppermute | solution.py:262
  64.7 1.3 %collective-permute-start.24 = (bf16[64,512]{1,0:T(8,128)(2,1)S(1)}, bf16[64,512]{1,0:T(8,128)(2,1)S(1)}, u32[]{:S(2)}, u32[]{:S(2)}) collective-permute-start(bf16[64,512]{1,0:T(8,128)(2,1)S(1)} %get-tuple-element.33), channel_id=1, source_target_pairs={{0,24},{8,16},{16,8},{24,0},{1,25},{9,17},{17,9},{25,1},{2,26},{10... | collective-permute-start | bytes 196616 | tf_op jit(solution)/shard_map/ppermute | solution.py:262
  65.9 2.6 %collective-permute-start.21 = (bf16[64,128]{1,0:T(8,128)(2,1)S(1)}, bf16[64,128]{1,0:T(8,128)(2,1)S(1)}, u32[]{:S(2)}, u32[]{:S(2)}) collective-permute-start(bf16[64,128]{1,0:T(8,128)(2,1)S(1)} %get-tuple-element.29.rest_0_), channel_id=1, source_target_pairs={{0,24},{8,16},{16,8},{24,0},{1,25},{9,17},{17,9},{25,1},{2,26},{10... | collective-permute-start | bytes 49160 | tf_op jit(solution)/shard_map/ppermute | solution.py:262
  68.7 2.8 %collective-permute-done.23.refs_2_ = bf16[64,512]{1,0:T(8,128)(2,1)S(1)} collective-permute-done((bf16[64,512]{1,0:T(8,128)(2,1)S(1)}, bf16[64,512]{1,0:T(8,128)(2,1)S(1)}, u32[]{:S(2)}, u32[]{:S(2)}) %collective-permute-start.23) | collective-permute-done | bytes 65568 | tf_op jit(solution)/shard_map/ppermute | solution.py:262
  71.6 2.4 %collective-permute-start.27 = (bf16[64,512]{1,0:T(8,128)(2,1)S(1)}, bf16[64,512]{1,0:T(8,128)(2,1)S(1)}, u32[]{:S(2)}, u32[]{:S(2)}) collective-permute-start(bf16[64,512]{1,0:T(8,128)(2,1)S(1)} %shard_map.59.rest_0_), channel_id=1, source_target_pairs={{0,24},{8,16},{16,8},{24,0},{1,25},{9,17},{17,9},{25,1},{2,26},{10... | collective-permute-start | bytes 196616 | tf_op jit(solution)/shard_map/ppermute | solution.py:262
  74.0 1.2 %collective-permute-start.26 = (bf16[64,512]{1,0:T(8,128)(2,1)S(1)}, bf16[64,512]{1,0:T(8,128)(2,1)S(1)}, u32[]{:S(2)}, u32[]{:S(2)}) collective-permute-start(bf16[64,512]{1,0:T(8,128)(2,1)S(1)} %shard_map.59.rest_0_), channel_id=1, source_target_pairs={{0,16},{8,24},{16,0},{24,8},{1,17},{9,25},{17,1},{25,9},{2,18},{10... | collective-permute-start | bytes 196616 | tf_op jit(solution)/shard_map/ppermute | solution.py:262
  75.2 0.9 collective-permute-start.25
  76.1 4.5 %shard_map.58.left_ref = bf16[2048,64]{1,0:T(8,128)(2,1)S(1)} custom-call(s32[2]{0:T(128)S(1)} %pad_add_fusion.where_ref, bf16[64,1024]{1,0:T(8,128)(2,1)S(1)} %get-tuple-element.28.own_half_ref, bf16[64,1024]{1,0:T(8,128)(2,1)S(1)} %collective-permute-done.18.got_half_ref, bf16[64,128]{1,0:T(8,128)(2,1)S(1)} %get-tuple-element.29.rest_0_, ...), custom_call_target="tpu_custom_call" | custom-call | flops 5000000000 | bytes 589824 | tf_op jit(solution)/shard_map/pallas_call | solution.py:250
  80.7 8.4 %shard_map.60 = (bf16[2048,2048]{1,0:T(8,128)(2,1)}, bf16[2048,2048]{1,0:T(8,128)(2,1)}) custom-call(s32[2]{0:T(128)S(1)} %pad_add_fusion.where_ref, bf16[2048,2048]{1,0:T(8,128)(2,1)S(1)} %bitcast.5, bf16[2048,64]{1,0:T(8,128)(2,1)S(1)} %shard_map.58.left_ref, bf16[64,512]{1,0:T(8,128)(2,1)S(1)} %shard_map.59.rest_0_, ...), custom_call_target="tpu_custom_call" | custom-call | flops 536870912 | bytes 8388608 | tf_op jit(solution)/shard_map/pallas_call | solution.py:290
  (45 shorter events, 2.1 us)
Async XLA Ops:
  9.1 1.6 %collective-permute-start = (bf16[64,1152]{1,0:T(8,128)(2,1)S(1)}, bf16[64,1152]{1,0:T(8,128)(2,1)S(1)}, u32[]{:S(2)}, u32[]{:S(2)}) collective-permute-start(bf16[64,1152]{1,0:T(8,128)(2,1)S(1)} %get-tuple-element.19), channel_id=1, source_target_pairs={{0,1},{1,0},{2,3},{3,2},{4,5},{5,4},{6,7},{7,6},{8,9},{9,8},{10,11... | collective-permute-start | bytes 442376 | tf_op jit(solution)/shard_map/ppermute | solution.py:262
  10.8 8.5 %collective-permute-start.3 = (bf16[64,1152]{1,0:T(8,128)(2,1)S(1)}, bf16[64,1152]{1,0:T(8,128)(2,1)S(1)}, u32[]{:S(2)}, u32[]{:S(2)}) collective-permute-start(bf16[64,1152]{1,0:T(8,128)(2,1)S(1)} %shard_map.51.refs_0_), channel_id=1, source_target_pairs={{0,6},{1,7},{2,4},{3,5},{4,2},{5,3},{6,0},{7,1},{8,14},{9,15},{10,... | collective-permute-start | bytes 442376 | tf_op jit(solution)/shard_map/ppermute | solution.py:262
  14.6 7.3 %collective-permute-start.2 = (bf16[64,1152]{1,0:T(8,128)(2,1)S(1)}, bf16[64,1152]{1,0:T(8,128)(2,1)S(1)}, u32[]{:S(2)}, u32[]{:S(2)}) collective-permute-start(bf16[64,1152]{1,0:T(8,128)(2,1)S(1)} %shard_map.51.refs_0_), channel_id=1, source_target_pairs={{0,4},{1,5},{2,6},{3,7},{4,0},{5,1},{6,2},{7,3},{8,12},{9,13},{10,... | collective-permute-start | bytes 442376 | tf_op jit(solution)/shard_map/ppermute | solution.py:262
  15.1 7.1 %collective-permute-start.1 = (bf16[64,1152]{1,0:T(8,128)(2,1)S(1)}, bf16[64,1152]{1,0:T(8,128)(2,1)S(1)}, u32[]{:S(2)}, u32[]{:S(2)}) collective-permute-start(bf16[64,1152]{1,0:T(8,128)(2,1)S(1)} %shard_map.51.refs_0_), channel_id=1, source_target_pairs={{0,2},{1,3},{2,0},{3,1},{4,6},{5,7},{6,4},{7,5},{8,10},{9,11},{10,... | collective-permute-start | bytes 442376 | tf_op jit(solution)/shard_map/ppermute | solution.py:262
  22.5 15.2 %collective-permute-start.4 = (bf16[64,1024]{1,0:T(8,128)(2,1)S(1)}, bf16[64,1024]{1,0:T(8,128)(2,1)S(1)}, u32[]{:S(2)}, u32[]{:S(2)}) collective-permute-start(bf16[64,1024]{1,0:T(8,128)(2,1)S(1)} %get-tuple-element.20.own_half_ref), channel_id=1, source_target_pairs={{0,1},{1,0},{2,3},{3,2},{4,5},{5,4},{6,7},{7,6},{8,9},{9,8},{10,11... | collective-permute-start | bytes 393224 | tf_op jit(solution)/shard_map/ppermute | solution.py:262
  22.5 8.1 %collective-permute-start.8 = (bf16[64,512]{1,0:T(8,128)(2,1)S(1)}, bf16[64,512]{1,0:T(8,128)(2,1)S(1)}, u32[]{:S(2)}, u32[]{:S(2)}) collective-permute-start(bf16[64,512]{1,0:T(8,128)(2,1)S(1)} %get-tuple-element.23), channel_id=1, source_target_pairs={{0,8},{8,0},{16,24},{24,16},{1,9},{9,1},{17,25},{25,17},{2,10},{10... | collective-permute-start | bytes 196616 | tf_op jit(solution)/shard_map/ppermute | solution.py:262
  24.1 8.9 %collective-permute-start.9 = (bf16[64,512]{1,0:T(8,128)(2,1)S(1)}, bf16[64,512]{1,0:T(8,128)(2,1)S(1)}, u32[]{:S(2)}, u32[]{:S(2)}) collective-permute-start(bf16[64,512]{1,0:T(8,128)(2,1)S(1)} %get-tuple-element.24), channel_id=1, source_target_pairs={{0,16},{8,24},{16,0},{24,8},{1,17},{9,25},{17,1},{25,9},{2,18},{10... | collective-permute-start | bytes 196616 | tf_op jit(solution)/shard_map/ppermute | solution.py:262
  26.7 6.4 %collective-permute-start.10 = (bf16[64,512]{1,0:T(8,128)(2,1)S(1)}, bf16[64,512]{1,0:T(8,128)(2,1)S(1)}, u32[]{:S(2)}, u32[]{:S(2)}) collective-permute-start(bf16[64,512]{1,0:T(8,128)(2,1)S(1)} %get-tuple-element.25), channel_id=1, source_target_pairs={{0,24},{8,16},{16,8},{24,0},{1,25},{9,17},{17,9},{25,1},{2,26},{10... | collective-permute-start | bytes 196616 | tf_op jit(solution)/shard_map/ppermute | solution.py:262
  26.9 8.9 %collective-permute-start.7 = (bf16[64,128]{1,0:T(8,128)(2,1)S(1)}, bf16[64,128]{1,0:T(8,128)(2,1)S(1)}, u32[]{:S(2)}, u32[]{:S(2)}) collective-permute-start(bf16[64,128]{1,0:T(8,128)(2,1)S(1)} %get-tuple-element.21.rest_0_), channel_id=1, source_target_pairs={{0,24},{8,16},{16,8},{24,0},{1,25},{9,17},{17,9},{25,1},{2,26},{10... | collective-permute-start | bytes 49160 | tf_op jit(solution)/shard_map/ppermute | solution.py:262
  30.5 6.2 %collective-permute-start.6 = (bf16[64,128]{1,0:T(8,128)(2,1)S(1)}, bf16[64,128]{1,0:T(8,128)(2,1)S(1)}, u32[]{:S(2)}, u32[]{:S(2)}) collective-permute-start(bf16[64,128]{1,0:T(8,128)(2,1)S(1)} %get-tuple-element.21.rest_0_), channel_id=1, source_target_pairs={{0,16},{8,24},{16,0},{24,8},{1,17},{9,25},{17,1},{25,9},{2,18},{10... | collective-permute-start | bytes 49160 | tf_op jit(solution)/shard_map/ppermute | solution.py:262
  33.1 4.6 %collective-permute-start.5 = (bf16[64,128]{1,0:T(8,128)(2,1)S(1)}, bf16[64,128]{1,0:T(8,128)(2,1)S(1)}, u32[]{:S(2)}, u32[]{:S(2)}) collective-permute-start(bf16[64,128]{1,0:T(8,128)(2,1)S(1)} %get-tuple-element.21.rest_0_), channel_id=1, source_target_pairs={{0,8},{8,0},{16,24},{24,16},{1,9},{9,1},{17,25},{25,17},{2,10},{10... | collective-permute-start | bytes 49160 | tf_op jit(solution)/shard_map/ppermute | solution.py:262
  33.1 9.1 %slice-start = ((s8[8388608]{0:T(1024)(128)(4,1)}), s8[4194304]{0:T(1024)(128)(4,1)S(1)}, s32[]{:S(2)}) async-start(s8[8388608]{0:T(1024)(128)(4,1)} %bitcast.4), calls=%async_computation | async-start | bytes 8388608
  33.1 9.1 %slice-start.1 = ((s8[8388608]{0:T(1024)(128)(4,1)}), s8[4194304]{0:T(1024)(128)(4,1)S(1)}, s32[]{:S(2)}) async-start(s8[8388608]{0:T(1024)(128)(4,1)} %bitcast.4), calls=%async_computation.1 | async-start | bytes 8388608
  33.1 9.0 %copy-start = (bf16[2048,64]{0,1:T(8,128)(2,1)S(1)}, bf16[2048,64]{0,1:T(8,128)(2,1)}, u32[]{:S(2)}) copy-start(bf16[2048,64]{0,1:T(8,128)(2,1)} %param.4) | copy-start | bytes 786436
  33.1 9.0 %copy-start.1 = (bf16[2048,64]{0,1:T(8,128)(2,1)S(1)}, bf16[2048,64]{0,1:T(8,128)(2,1)}, u32[]{:S(2)}) copy-start(bf16[2048,64]{0,1:T(8,128)(2,1)} %param.5) | copy-start | bytes 786436
  33.2 9.0 %collective-permute-start.13 = (bf16[64,512]{1,0:T(8,128)(2,1)S(1)}, bf16[64,512]{1,0:T(8,128)(2,1)S(1)}, u32[]{:S(2)}, u32[]{:S(2)}) collective-permute-start(bf16[64,512]{1,0:T(8,128)(2,1)S(1)} %shard_map.54.rest_0_), channel_id=1, source_target_pairs={{0,24},{8,16},{16,8},{24,0},{1,25},{9,17},{17,9},{25,1},{2,26},{10... | collective-permute-start | bytes 196616 | tf_op jit(solution)/shard_map/ppermute | solution.py:262
  35.8 6.4 %collective-permute-start.12 = (bf16[64,512]{1,0:T(8,128)(2,1)S(1)}, bf16[64,512]{1,0:T(8,128)(2,1)S(1)}, u32[]{:S(2)}, u32[]{:S(2)}) collective-permute-start(bf16[64,512]{1,0:T(8,128)(2,1)S(1)} %shard_map.54.rest_0_), channel_id=1, source_target_pairs={{0,16},{8,24},{16,0},{24,8},{1,17},{9,25},{17,1},{25,9},{2,18},{10... | collective-permute-start | bytes 196616 | tf_op jit(solution)/shard_map/ppermute | solution.py:262
  36.7 5.4 %collective-permute-start.11 = (bf16[64,512]{1,0:T(8,128)(2,1)S(1)}, bf16[64,512]{1,0:T(8,128)(2,1)S(1)}, u32[]{:S(2)}, u32[]{:S(2)}) collective-permute-start(bf16[64,512]{1,0:T(8,128)(2,1)S(1)} %shard_map.54.rest_0_), channel_id=1, source_target_pairs={{0,8},{8,0},{16,24},{24,16},{1,9},{9,1},{17,25},{25,17},{2,10},{10... | collective-permute-start | bytes 196616 | tf_op jit(solution)/shard_map/ppermute | solution.py:262
  49.7 1.4 %collective-permute-start.14 = (bf16[64,1152]{1,0:T(8,128)(2,1)S(1)}, bf16[64,1152]{1,0:T(8,128)(2,1)S(1)}, u32[]{:S(2)}, u32[]{:S(2)}) collective-permute-start(bf16[64,1152]{1,0:T(8,128)(2,1)S(1)} %get-tuple-element.27), channel_id=1, source_target_pairs={{0,1},{1,0},{2,3},{3,2},{4,5},{5,4},{6,7},{7,6},{8,9},{9,8},{10,11... | collective-permute-start | bytes 442376 | tf_op jit(solution)/shard_map/ppermute | solution.py:262
  51.3 7.7 %collective-permute-start.17 = (bf16[64,1152]{1,0:T(8,128)(2,1)S(1)}, bf16[64,1152]{1,0:T(8,128)(2,1)S(1)}, u32[]{:S(2)}, u32[]{:S(2)}) collective-permute-start(bf16[64,1152]{1,0:T(8,128)(2,1)S(1)} %shard_map.56.refs_0_), channel_id=1, source_target_pairs={{0,6},{1,7},{2,4},{3,5},{4,2},{5,3},{6,0},{7,1},{8,14},{9,15},{10,... | collective-permute-start | bytes 442376 | tf_op jit(solution)/shard_map/ppermute | solution.py:262
  52.9 8.3 %collective-permute-start.16 = (bf16[64,1152]{1,0:T(8,128)(2,1)S(1)}, bf16[64,1152]{1,0:T(8,128)(2,1)S(1)}, u32[]{:S(2)}, u32[]{:S(2)}) collective-permute-start(bf16[64,1152]{1,0:T(8,128)(2,1)S(1)} %shard_map.56.refs_0_), channel_id=1, source_target_pairs={{0,4},{1,5},{2,6},{3,7},{4,0},{5,1},{6,2},{7,3},{8,12},{9,13},{10,... | collective-permute-start | bytes 442376 | tf_op jit(solution)/shard_map/ppermute | solution.py:262
  54.2 7.0 %collective-permute-start.15 = (bf16[64,1152]{1,0:T(8,128)(2,1)S(1)}, bf16[64,1152]{1,0:T(8,128)(2,1)S(1)}, u32[]{:S(2)}, u32[]{:S(2)}) collective-permute-start(bf16[64,1152]{1,0:T(8,128)(2,1)S(1)} %shard_map.56.refs_0_), channel_id=1, source_target_pairs={{0,2},{1,3},{2,0},{3,1},{4,6},{5,7},{6,4},{7,5},{8,10},{9,11},{10,... | collective-permute-start | bytes 442376 | tf_op jit(solution)/shard_map/ppermute | solution.py:262
  61.5 14.6 %collective-permute-start.18 = (bf16[64,1024]{1,0:T(8,128)(2,1)S(1)}, bf16[64,1024]{1,0:T(8,128)(2,1)S(1)}, u32[]{:S(2)}, u32[]{:S(2)}) collective-permute-start(bf16[64,1024]{1,0:T(8,128)(2,1)S(1)} %get-tuple-element.28.own_half_ref), channel_id=1, source_target_pairs={{0,1},{1,0},{2,3},{3,2},{4,5},{5,4},{6,7},{7,6},{8,9},{9,8},{10,11... | collective-permute-start | bytes 393224 | tf_op jit(solution)/shard_map/ppermute | solution.py:262
  61.5 7.0 %collective-permute-start.22 = (bf16[64,512]{1,0:T(8,128)(2,1)S(1)}, bf16[64,512]{1,0:T(8,128)(2,1)S(1)}, u32[]{:S(2)}, u32[]{:S(2)}) collective-permute-start(bf16[64,512]{1,0:T(8,128)(2,1)S(1)} %get-tuple-element.31), channel_id=1, source_target_pairs={{0,8},{8,0},{16,24},{24,16},{1,9},{9,1},{17,25},{25,17},{2,10},{10... | collective-permute-start | bytes 196616 | tf_op jit(solution)/shard_map/ppermute | solution.py:262
  62.7 8.9 %collective-permute-start.23 = (bf16[64,512]{1,0:T(8,128)(2,1)S(1)}, bf16[64,512]{1,0:T(8,128)(2,1)S(1)}, u32[]{:S(2)}, u32[]{:S(2)}) collective-permute-start(bf16[64,512]{1,0:T(8,128)(2,1)S(1)} %get-tuple-element.32), channel_id=1, source_target_pairs={{0,16},{8,24},{16,0},{24,8},{1,17},{9,25},{17,1},{25,9},{2,18},{10... | collective-permute-start | bytes 196616 | tf_op jit(solution)/shard_map/ppermute | solution.py:262
  64.7 6.9 %collective-permute-start.24 = (bf16[64,512]{1,0:T(8,128)(2,1)S(1)}, bf16[64,512]{1,0:T(8,128)(2,1)S(1)}, u32[]{:S(2)}, u32[]{:S(2)}) collective-permute-start(bf16[64,512]{1,0:T(8,128)(2,1)S(1)} %get-tuple-element.33), channel_id=1, source_target_pairs={{0,24},{8,16},{16,8},{24,0},{1,25},{9,17},{17,9},{25,1},{2,26},{10... | collective-permute-start | bytes 196616 | tf_op jit(solution)/shard_map/ppermute | solution.py:262
  65.9 8.1 %collective-permute-start.21 = (bf16[64,128]{1,0:T(8,128)(2,1)S(1)}, bf16[64,128]{1,0:T(8,128)(2,1)S(1)}, u32[]{:S(2)}, u32[]{:S(2)}) collective-permute-start(bf16[64,128]{1,0:T(8,128)(2,1)S(1)} %get-tuple-element.29.rest_0_), channel_id=1, source_target_pairs={{0,24},{8,16},{16,8},{24,0},{1,25},{9,17},{17,9},{25,1},{2,26},{10... | collective-permute-start | bytes 49160 | tf_op jit(solution)/shard_map/ppermute | solution.py:262
  68.5 6.7 %collective-permute-start.20 = (bf16[64,128]{1,0:T(8,128)(2,1)S(1)}, bf16[64,128]{1,0:T(8,128)(2,1)S(1)}, u32[]{:S(2)}, u32[]{:S(2)}) collective-permute-start(bf16[64,128]{1,0:T(8,128)(2,1)S(1)} %get-tuple-element.29.rest_0_), channel_id=1, source_target_pairs={{0,16},{8,24},{16,0},{24,8},{1,17},{9,25},{17,1},{25,9},{2,18},{10... | collective-permute-start | bytes 49160 | tf_op jit(solution)/shard_map/ppermute | solution.py:262
  71.6 4.5 %collective-permute-start.19 = (bf16[64,128]{1,0:T(8,128)(2,1)S(1)}, bf16[64,128]{1,0:T(8,128)(2,1)S(1)}, u32[]{:S(2)}, u32[]{:S(2)}) collective-permute-start(bf16[64,128]{1,0:T(8,128)(2,1)S(1)} %get-tuple-element.29.rest_0_), channel_id=1, source_target_pairs={{0,8},{8,0},{16,24},{24,16},{1,9},{9,1},{17,25},{25,17},{2,10},{10... | collective-permute-start | bytes 49160 | tf_op jit(solution)/shard_map/ppermute | solution.py:262
  71.6 9.0 %collective-permute-start.27 = (bf16[64,512]{1,0:T(8,128)(2,1)S(1)}, bf16[64,512]{1,0:T(8,128)(2,1)S(1)}, u32[]{:S(2)}, u32[]{:S(2)}) collective-permute-start(bf16[64,512]{1,0:T(8,128)(2,1)S(1)} %shard_map.59.rest_0_), channel_id=1, source_target_pairs={{0,24},{8,16},{16,8},{24,0},{1,25},{9,17},{17,9},{25,1},{2,26},{10... | collective-permute-start | bytes 196616 | tf_op jit(solution)/shard_map/ppermute | solution.py:262
  74.0 6.7 %collective-permute-start.26 = (bf16[64,512]{1,0:T(8,128)(2,1)S(1)}, bf16[64,512]{1,0:T(8,128)(2,1)S(1)}, u32[]{:S(2)}, u32[]{:S(2)}) collective-permute-start(bf16[64,512]{1,0:T(8,128)(2,1)S(1)} %shard_map.59.rest_0_), channel_id=1, source_target_pairs={{0,16},{8,24},{16,0},{24,8},{1,17},{9,25},{17,1},{25,9},{2,18},{10... | collective-permute-start | bytes 196616 | tf_op jit(solution)/shard_map/ppermute | solution.py:262
  75.2 5.4 %collective-permute-start.25 = (bf16[64,512]{1,0:T(8,128)(2,1)S(1)}, bf16[64,512]{1,0:T(8,128)(2,1)S(1)}, u32[]{:S(2)}, u32[]{:S(2)}) collective-permute-start(bf16[64,512]{1,0:T(8,128)(2,1)S(1)} %shard_map.59.rest_0_), channel_id=1, source_target_pairs={{0,8},{8,0},{16,24},{24,16},{1,9},{9,1},{17,25},{25,17},{2,10},{10... | collective-permute-start | bytes 196616 | tf_op jit(solution)/shard_map/ppermute | solution.py:262
where the time goes:
time: 89.2 us; the launch traced here: 89 us
  Pallas kernels  34 us (38%)
  starting transfers between devices  32.8 us (37%)
  waiting for transfers between devices  21.3 us (24%)
    ppermute x28, starting transfers between devices, exchange(): return lax.ppermute(x, axis, [(i, i ^ k) for i in range(size)])  32.8 us
    pallas_call x3, Pallas kernels, run(): pl.pallas_call(kernel, grid_spec=pltpu.PrefetchScalarGridSpec(num_scalar_...  24.2 us
    ppermute x28, waiting for transfers between devices, exchange(): return lax.ppermute(x, axis, [(i, i ^ k) for i in range(size)])  21.3 us
    pallas_call x8, Pallas kernels, vmem_call(): pl.pallas_call(kernel, out_shape=outs, in_specs=([] if where is None else...  9.87 us
  transfers between devices with their start and end apart: 28, of which 10 were waited for; matrix products, arithmetic and copies ran while one was open for 0% of the time, Pallas kernels for 10%

commit v1 on v0

--- a/solution.py
+++ b/solution.py
@@ -46,7 +46,8 @@
     high, rest = split2(y2)
     low = (y2 - high.astype(F32) - rest.astype(F32)).astype(BF16)
     vp = vpt_ref[...]
-    core = sum(dot(part, vp, ((1,), (1,))) for part in (high, rest, low))
+    parts = dot(jnp.concatenate([high, rest, low], axis=0), vp, ((1,), (1,)))
+    core = parts[:rank] + parts[rank : 2 * rank] + parts[2 * rank :]
     side = where_ref[0]
     row = where_ref[1]
     own_ref[:, :half] = y1_scr[:, pl.ds(pl.multiple_of(side * half, LANES), half)]
@@ -269,7 +270,8 @@
     half, share = frames // 2, voxels // n_row
     width = half + 2 * rank
     rows = min(512, frames)
-    last_rows = min(256, frames)
+    mid_rows = min(1024, frames)
+    last_rows = min(512, frames)
     chunk = min(256, voxels)
     where = jnp.stack([lax.axis_index("vox") % 2, lax.axis_index("frm")]).astype(jnp.int32)
     vpt, fpt = voxel_probe.T, frame_probe.T
@@ -343,11 +345,11 @@
     for _ in range(1, ITERS):
         sketch = run(
             functools.partial(middle_kernel, n_row, chunk),
-            frames // rows,
-            [resident] + probe_specs + side_specs,
+            frames // mid_rows,
+            [resident, resident, block_cols(rank, mid_rows)] + side_specs,
             sketch_specs,
             sketch_shapes,
-            [right, pltpu.VMEM((rows, voxels), BF16)] + sums,
+            [right, pltpu.VMEM((mid_rows, voxels), BF16)] + sums,
             3,
             (movie, vpt, fpt, *sides),
         )
@@ -355,7 +357,7 @@
     out = jax.ShapeDtypeStruct((frames, voxels), BF16)
     return tuple(
         run(
-            functools.partial(last_kernel, n_row, chunk),
+            functools.partial(last_kernel, n_row, 256),
             frames // last_rows,
             [resident] + side_specs,
             [block_rows(last_rows, voxels)] * 2,

time: 89.2 us -> 87.9 us (0.985)
  Pallas kernels: 34 us -> 32.8 us
    pallas_call x3, Pallas kernels: 24.2 us -> 22.9 us  [run(): pl.pallas_call(kernel, grid_spec=pltpu.PrefetchScalarGridSpec(num_scalar_...]
where the time goes in v1:
time: 87.9 us; the launch traced here: 87.8 us
  Pallas kernels  32.8 us (37%)
  starting transfers between devices  32.8 us (37%)
  waiting for transfers between devices  21.3 us (24%)
    ppermute x28, starting transfers between devices, exchange(): return lax.ppermute(x, axis, [(i, i ^ k) for i in range(size)])  32.8 us
    pallas_call x3, Pallas kernels, run(): pl.pallas_call(kernel, grid_spec=pltpu.PrefetchScalarGridSpec(num_scalar_...  22.9 us
    ppermute x28, waiting for transfers between devices, exchange(): return lax.ppermute(x, axis, [(i, i ^ k) for i in range(size)])  21.3 us
    pallas_call x8, Pallas kernels, vmem_call(): pl.pallas_call(kernel, out_shape=outs, in_specs=([] if where is None else...  9.87 us
  transfers between devices with their start and end apart: 28, of which 10 were waited for; matrix products, arithmetic and copies ran while one was open for 0% of the time, Pallas kernels for 10%

profile of v1, /device:TPU:0, one launch (start us, length us, event | category | flops | bytes accessed | tf_op | source)
XLA Modules:
  0.0 87.8 jit_solution(11700103777214333206)
XLA Ops:
  0.7 8.3 %shard_map.50 = (f32[64,1152]{1,0:T(8,128)S(1)}, bf16[64,1152]{1,0:T(8,128)(2,1)S(1)}, f32[64,512]{1,0:T(8,128)S(1)}, bf16[64,512]{1,0:T(8,128)(2,1)S(1)}, bf16[...) custom-call(s32[2]{0:T(128)S(1)} %pad_add_fusion.where_ref, bf16[2048,2048]{1,0:T(8,128)(2,1)} %movie_ref.5, ...), custom_call_target="tpu_custom_call" | custom-call | flops 1073741824 | bytes 8388608 | tf_op jit(solution)/shard_map/pallas_call | solution.py:292
  9.1 0.6 collective-permute-start
  9.6 1.0 %collective-permute-done.got_ref = bf16[64,1152]{1,0:T(8,128)(2,1)S(1)} collective-permute-done((bf16[64,1152]{1,0:T(8,128)(2,1)S(1)}, bf16[64,1152]{1,0:T(8,128)(2,1)S(1)}, u32[]{:S(2)}, u32[]{:S(2)}) %collective-permute-start) | collective-permute-done | bytes 147488 | tf_op jit(solution)/shard_map/ppermute | solution.py:263
  10.8 3.8 %collective-permute-start.3 = (bf16[64,1152]{1,0:T(8,128)(2,1)S(1)}, bf16[64,1152]{1,0:T(8,128)(2,1)S(1)}, u32[]{:S(2)}, u32[]{:S(2)}) collective-permute-start(bf16[64,1152]{1,0:T(8,128)(2,1)S(1)} %shard_map.51.refs_0_), channel_id=1, source_target_pairs={{0,6},{1,7},{2,4},{3,5},{4,2},{5,3},{6,0},{7,1},{8,14},{9,15},{10,... | collective-permute-start | bytes 442376 | tf_op jit(solution)/shard_map/ppermute | solution.py:263
  14.6 0.5 collective-permute-start.2
  15.2 4.0 %collective-permute-done.3.refs_3_ = bf16[64,1152]{1,0:T(8,128)(2,1)S(1)} collective-permute-done((bf16[64,1152]{1,0:T(8,128)(2,1)S(1)}, bf16[64,1152]{1,0:T(8,128)(2,1)S(1)}, u32[]{:S(2)}, u32[]{:S(2)}) %collective-permute-start.3) | collective-permute-done | bytes 147488 | tf_op jit(solution)/shard_map/ppermute | solution.py:263
  19.3 2.6 %collective-permute-done.2.refs_2_ = bf16[64,1152]{1,0:T(8,128)(2,1)S(1)} collective-permute-done((bf16[64,1152]{1,0:T(8,128)(2,1)S(1)}, bf16[64,1152]{1,0:T(8,128)(2,1)S(1)}, u32[]{:S(2)}, u32[]{:S(2)}) %collective-permute-start.2) | collective-permute-done | bytes 147488 | tf_op jit(solution)/shard_map/ppermute | solution.py:263
  22.5 1.6 %collective-permute-start.8 = (bf16[64,512]{1,0:T(8,128)(2,1)S(1)}, bf16[64,512]{1,0:T(8,128)(2,1)S(1)}, u32[]{:S(2)}, u32[]{:S(2)}) collective-permute-start(bf16[64,512]{1,0:T(8,128)(2,1)S(1)} %get-tuple-element.23), channel_id=1, source_target_pairs={{0,8},{8,0},{16,24},{24,16},{1,9},{9,1},{17,25},{25,17},{2,10},{10... | collective-permute-start | bytes 196616 | tf_op jit(solution)/shard_map/ppermute | solution.py:263
  24.1 2.6 %collective-permute-start.9 = (bf16[64,512]{1,0:T(8,128)(2,1)S(1)}, bf16[64,512]{1,0:T(8,128)(2,1)S(1)}, u32[]{:S(2)}, u32[]{:S(2)}) collective-permute-start(bf16[64,512]{1,0:T(8,128)(2,1)S(1)} %get-tuple-element.24), channel_id=1, source_target_pairs={{0,16},{8,24},{16,0},{24,8},{1,17},{9,25},{17,1},{25,9},{2,18},{10... | collective-permute-start | bytes 196616 | tf_op jit(solution)/shard_map/ppermute | solution.py:263
  26.9 3.6 %collective-permute-start.7 = (bf16[64,128]{1,0:T(8,128)(2,1)S(1)}, bf16[64,128]{1,0:T(8,128)(2,1)S(1)}, u32[]{:S(2)}, u32[]{:S(2)}) collective-permute-start(bf16[64,128]{1,0:T(8,128)(2,1)S(1)} %get-tuple-element.21.rest_0_), channel_id=1, source_target_pairs={{0,24},{8,16},{16,8},{24,0},{1,25},{9,17},{17,9},{25,1},{2,26},{10... | collective-permute-start | bytes 49160 | tf_op jit(solution)/shard_map/ppermute | solution.py:263
  30.5 2.5 %collective-permute-done.9.refs_2_ = bf16[64,512]{1,0:T(8,128)(2,1)S(1)} collective-permute-done((bf16[64,512]{1,0:T(8,128)(2,1)S(1)}, bf16[64,512]{1,0:T(8,128)(2,1)S(1)}, u32[]{:S(2)}, u32[]{:S(2)}) %collective-permute-start.9) | collective-permute-done | bytes 65568 | tf_op jit(solution)/shard_map/ppermute | solution.py:263
  33.1 2.6 %collective-permute-start.13 = (bf16[64,512]{1,0:T(8,128)(2,1)S(1)}, bf16[64,512]{1,0:T(8,128)(2,1)S(1)}, u32[]{:S(2)}, u32[]{:S(2)}) collective-permute-start(bf16[64,512]{1,0:T(8,128)(2,1)S(1)} %shard_map.54.rest_0_), channel_id=1, source_target_pairs={{0,24},{8,16},{16,8},{24,0},{1,25},{9,17},{17,9},{25,1},{2,26},{10... | collective-permute-start | bytes 196616 | tf_op jit(solution)/shard_map/ppermute | solution.py:263
  35.8 0.9 %collective-permute-start.12 = (bf16[64,512]{1,0:T(8,128)(2,1)S(1)}, bf16[64,512]{1,0:T(8,128)(2,1)S(1)}, u32[]{:S(2)}, u32[]{:S(2)}) collective-permute-start(bf16[64,512]{1,0:T(8,128)(2,1)S(1)} %shard_map.54.rest_0_), channel_id=1, source_target_pairs={{0,16},{8,24},{16,0},{24,8},{1,17},{9,25},{17,1},{25,9},{2,18},{10... | collective-permute-start | bytes 196616 | tf_op jit(solution)/shard_map/ppermute | solution.py:263
  36.7 0.9 %collective-permute-start.11 = (bf16[64,512]{1,0:T(8,128)(2,1)S(1)}, bf16[64,512]{1,0:T(8,128)(2,1)S(1)}, u32[]{:S(2)}, u32[]{:S(2)}) collective-permute-start(bf16[64,512]{1,0:T(8,128)(2,1)S(1)} %shard_map.54.rest_0_), channel_id=1, source_target_pairs={{0,8},{8,0},{16,24},{24,16},{1,9},{9,1},{17,25},{25,17},{2,10},{10... | collective-permute-start | bytes 196616 | tf_op jit(solution)/shard_map/ppermute | solution.py:263
  37.6 4.5 %shard_map.53.left_ref = bf16[2048,64]{1,0:T(8,128)(2,1)S(1)} custom-call(s32[2]{0:T(128)S(1)} %pad_add_fusion.where_ref, bf16[64,1024]{1,0:T(8,128)(2,1)S(1)} %get-tuple-element.20.own_half_ref, bf16[64,1024]{1,0:T(8,128)(2,1)S(1)} %collective-permute-done.4.got_half_ref, bf16[64,128]{1,0:T(8,128)(2,1)S(1)} %get-tuple-element.21.rest_0_, ...), custom_call_target="tpu_custom_call" | custom-call | flops 5000000000 | bytes 589824 | tf_op jit(solution)/shard_map/pallas_call | solution.py:251
  42.2 7.0 %shard_map.55 = (f32[64,1152]{1,0:T(8,128)S(1)}, bf16[64,1152]{1,0:T(8,128)(2,1)S(1)}, f32[64,512]{1,0:T(8,128)S(1)}, bf16[64,512]{1,0:T(8,128)(2,1)S(1)}, bf16[...) custom-call(s32[2]{0:T(128)S(1)} %pad_add_fusion.where_ref, bf16[2048,2048]{1,0:T(8,128)(2,1)S(1)} %bitcast.5, ...), custom_call_target="tpu_custom_call" | custom-call | flops 1610612736 | bytes 8388608 | tf_op jit(solution)/shard_map/pallas_call | solution.py:292
  49.2 1.4 %collective-permute-done.14.got_ref = bf16[64,1152]{1,0:T(8,128)(2,1)S(1)} collective-permute-done((bf16[64,1152]{1,0:T(8,128)(2,1)S(1)}, bf16[64,1152]{1,0:T(8,128)(2,1)S(1)}, u32[]{:S(2)}, u32[]{:S(2)}) %collective-permute-start.14) | collective-permute-done | bytes 147488 | tf_op jit(solution)/shard_map/ppermute | solution.py:263
  50.7 1.7 %collective-permute-start.17 = (bf16[64,1152]{1,0:T(8,128)(2,1)S(1)}, bf16[64,1152]{1,0:T(8,128)(2,1)S(1)}, u32[]{:S(2)}, u32[]{:S(2)}) collective-permute-start(bf16[64,1152]{1,0:T(8,128)(2,1)S(1)} %shard_map.56.refs_0_), channel_id=1, source_target_pairs={{0,6},{1,7},{2,4},{3,5},{4,2},{5,3},{6,0},{7,1},{8,14},{9,15},{10,... | collective-permute-start | bytes 442376 | tf_op jit(solution)/shard_map/ppermute | solution.py:263
  52.4 1.3 %collective-permute-start.16 = (bf16[64,1152]{1,0:T(8,128)(2,1)S(1)}, bf16[64,1152]{1,0:T(8,128)(2,1)S(1)}, u32[]{:S(2)}, u32[]{:S(2)}) collective-permute-start(bf16[64,1152]{1,0:T(8,128)(2,1)S(1)} %shard_map.56.refs_0_), channel_id=1, source_target_pairs={{0,4},{1,5},{2,6},{3,7},{4,0},{5,1},{6,2},{7,3},{8,12},{9,13},{10,... | collective-permute-start | bytes 442376 | tf_op jit(solution)/shard_map/ppermute | solution.py:263
  53.7 0.5 collective-permute-start.15
  54.2 4.2 %collective-permute-done.17.refs_3_ = bf16[64,1152]{1,0:T(8,128)(2,1)S(1)} collective-permute-done((bf16[64,1152]{1,0:T(8,128)(2,1)S(1)}, bf16[64,1152]{1,0:T(8,128)(2,1)S(1)}, u32[]{:S(2)}, u32[]{:S(2)}) %collective-permute-start.17) | collective-permute-done | bytes 147488 | tf_op jit(solution)/shard_map/ppermute | solution.py:263
  58.4 2.3 %collective-permute-done.16.refs_2_ = bf16[64,1152]{1,0:T(8,128)(2,1)S(1)} collective-permute-done((bf16[64,1152]{1,0:T(8,128)(2,1)S(1)}, bf16[64,1152]{1,0:T(8,128)(2,1)S(1)}, u32[]{:S(2)}, u32[]{:S(2)}) %collective-permute-start.16) | collective-permute-done | bytes 147488 | tf_op jit(solution)/shard_map/ppermute | solution.py:263
  61.0 1.2 %collective-permute-start.22 = (bf16[64,512]{1,0:T(8,128)(2,1)S(1)}, bf16[64,512]{1,0:T(8,128)(2,1)S(1)}, u32[]{:S(2)}, u32[]{:S(2)}) collective-permute-start(bf16[64,512]{1,0:T(8,128)(2,1)S(1)} %get-tuple-element.31), channel_id=1, source_target_pairs={{0,8},{8,0},{16,24},{24,16},{1,9},{9,1},{17,25},{25,17},{2,10},{10... | collective-permute-start | bytes 196616 | tf_op jit(solution)/shard_map/ppermute | solution.py:263
  62.2 2.0 %collective-permute-start.23 = (bf16[64,512]{1,0:T(8,128)(2,1)S(1)}, bf16[64,512]{1,0:T(8,128)(2,1)S(1)}, u32[]{:S(2)}, u32[]{:S(2)}) collective-permute-start(bf16[64,512]{1,0:T(8,128)(2,1)S(1)} %get-tuple-element.32), channel_id=1, source_target_pairs={{0,16},{8,24},{16,0},{24,8},{1,17},{9,25},{17,1},{25,9},{2,18},{10... | collective-permute-start | bytes 196616 | tf_op jit(solution)/shard_map/ppermute | solution.py:263
  64.2 1.3 %collective-permute-start.24 = (bf16[64,512]{1,0:T(8,128)(2,1)S(1)}, bf16[64,512]{1,0:T(8,128)(2,1)S(1)}, u32[]{:S(2)}, u32[]{:S(2)}) collective-permute-start(bf16[64,512]{1,0:T(8,128)(2,1)S(1)} %get-tuple-element.33), channel_id=1, source_target_pairs={{0,24},{8,16},{16,8},{24,0},{1,25},{9,17},{17,9},{25,1},{2,26},{10... | collective-permute-start | bytes 196616 | tf_op jit(solution)/shard_map/ppermute | solution.py:263
  65.4 2.6 %collective-permute-start.21 = (bf16[64,128]{1,0:T(8,128)(2,1)S(1)}, bf16[64,128]{1,0:T(8,128)(2,1)S(1)}, u32[]{:S(2)}, u32[]{:S(2)}) collective-permute-start(bf16[64,128]{1,0:T(8,128)(2,1)S(1)} %get-tuple-element.29.rest_0_), channel_id=1, source_target_pairs={{0,24},{8,16},{16,8},{24,0},{1,25},{9,17},{17,9},{25,1},{2,26},{10... | collective-permute-start | bytes 49160 | tf_op jit(solution)/shard_map/ppermute | solution.py:263
  68.2 2.8 %collective-permute-done.23.refs_2_ = bf16[64,512]{1,0:T(8,128)(2,1)S(1)} collective-permute-done((bf16[64,512]{1,0:T(8,128)(2,1)S(1)}, bf16[64,512]{1,0:T(8,128)(2,1)S(1)}, u32[]{:S(2)}, u32[]{:S(2)}) %collective-permute-start.23) | collective-permute-done | bytes 65568 | tf_op jit(solution)/shard_map/ppermute | solution.py:263
  71.1 2.4 %collective-permute-start.27 = (bf16[64,512]{1,0:T(8,128)(2,1)S(1)}, bf16[64,512]{1,0:T(8,128)(2,1)S(1)}, u32[]{:S(2)}, u32[]{:S(2)}) collective-permute-start(bf16[64,512]{1,0:T(8,128)(2,1)S(1)} %shard_map.59.rest_0_), channel_id=1, source_target_pairs={{0,24},{8,16},{16,8},{24,0},{1,25},{9,17},{17,9},{25,1},{2,26},{10... | collective-permute-start | bytes 196616 | tf_op jit(solution)/shard_map/ppermute | solution.py:263
  73.5 1.2 %collective-permute-start.26 = (bf16[64,512]{1,0:T(8,128)(2,1)S(1)}, bf16[64,512]{1,0:T(8,128)(2,1)S(1)}, u32[]{:S(2)}, u32[]{:S(2)}) collective-permute-start(bf16[64,512]{1,0:T(8,128)(2,1)S(1)} %shard_map.59.rest_0_), channel_id=1, source_target_pairs={{0,16},{8,24},{16,0},{24,8},{1,17},{9,25},{17,1},{25,9},{2,18},{10... | collective-permute-start | bytes 196616 | tf_op jit(solution)/shard_map/ppermute | solution.py:263
  74.7 0.9 collective-permute-start.25
  75.6 4.5 %shard_map.58.left_ref = bf16[2048,64]{1,0:T(8,128)(2,1)S(1)} custom-call(s32[2]{0:T(128)S(1)} %pad_add_fusion.where_ref, bf16[64,1024]{1,0:T(8,128)(2,1)S(1)} %get-tuple-element.28.own_half_ref, bf16[64,1024]{1,0:T(8,128)(2,1)S(1)} %collective-permute-done.18.got_half_ref, bf16[64,128]{1,0:T(8,128)(2,1)S(1)} %get-tuple-element.29.rest_0_, ...), custom_call_target="tpu_custom_call" | custom-call | flops 5000000000 | bytes 589824 | tf_op jit(solution)/shard_map/pallas_call | solution.py:251
  80.2 7.6 %shard_map.60 = (bf16[2048,2048]{1,0:T(8,128)(2,1)}, bf16[2048,2048]{1,0:T(8,128)(2,1)}) custom-call(s32[2]{0:T(128)S(1)} %pad_add_fusion.where_ref, bf16[2048,2048]{1,0:T(8,128)(2,1)S(1)} %bitcast.5, bf16[2048,64]{1,0:T(8,128)(2,1)S(1)} %shard_map.58.left_ref, bf16[64,512]{1,0:T(8,128)(2,1)S(1)} %shard_map.59.rest_0_, ...), custom_call_target="tpu_custom_call" | custom-call | flops 536870912 | bytes 8388608 | tf_op jit(solution)/shard_map/pallas_call | solution.py:292
  (45 shorter events, 2.1 us)
Async XLA Ops:
  9.1 1.6 %collective-permute-start = (bf16[64,1152]{1,0:T(8,128)(2,1)S(1)}, bf16[64,1152]{1,0:T(8,128)(2,1)S(1)}, u32[]{:S(2)}, u32[]{:S(2)}) collective-permute-start(bf16[64,1152]{1,0:T(8,128)(2,1)S(1)} %get-tuple-element.19), channel_id=1, source_target_pairs={{0,1},{1,0},{2,3},{3,2},{4,5},{5,4},{6,7},{7,6},{8,9},{9,8},{10,11... | collective-permute-start | bytes 442376 | tf_op jit(solution)/shard_map/ppermute | solution.py:263
  10.8 8.5 %collective-permute-start.3 = (bf16[64,1152]{1,0:T(8,128)(2,1)S(1)}, bf16[64,1152]{1,0:T(8,128)(2,1)S(1)}, u32[]{:S(2)}, u32[]{:S(2)}) collective-permute-start(bf16[64,1152]{1,0:T(8,128)(2,1)S(1)} %shard_map.51.refs_0_), channel_id=1, source_target_pairs={{0,6},{1,7},{2,4},{3,5},{4,2},{5,3},{6,0},{7,1},{8,14},{9,15},{10,... | collective-permute-start | bytes 442376 | tf_op jit(solution)/shard_map/ppermute | solution.py:263
  14.6 7.3 %collective-permute-start.2 = (bf16[64,1152]{1,0:T(8,128)(2,1)S(1)}, bf16[64,1152]{1,0:T(8,128)(2,1)S(1)}, u32[]{:S(2)}, u32[]{:S(2)}) collective-permute-start(bf16[64,1152]{1,0:T(8,128)(2,1)S(1)} %shard_map.51.refs_0_), channel_id=1, source_target_pairs={{0,4},{1,5},{2,6},{3,7},{4,0},{5,1},{6,2},{7,3},{8,12},{9,13},{10,... | collective-permute-start | bytes 442376 | tf_op jit(solution)/shard_map/ppermute | solution.py:263
  15.1 7.1 %collective-permute-start.1 = (bf16[64,1152]{1,0:T(8,128)(2,1)S(1)}, bf16[64,1152]{1,0:T(8,128)(2,1)S(1)}, u32[]{:S(2)}, u32[]{:S(2)}) collective-permute-start(bf16[64,1152]{1,0:T(8,128)(2,1)S(1)} %shard_map.51.refs_0_), channel_id=1, source_target_pairs={{0,2},{1,3},{2,0},{3,1},{4,6},{5,7},{6,4},{7,5},{8,10},{9,11},{10,... | collective-permute-start | bytes 442376 | tf_op jit(solution)/shard_map/ppermute | solution.py:263
  22.4 15.2 %collective-permute-start.4 = (bf16[64,1024]{1,0:T(8,128)(2,1)S(1)}, bf16[64,1024]{1,0:T(8,128)(2,1)S(1)}, u32[]{:S(2)}, u32[]{:S(2)}) collective-permute-start(bf16[64,1024]{1,0:T(8,128)(2,1)S(1)} %get-tuple-element.20.own_half_ref), channel_id=1, source_target_pairs={{0,1},{1,0},{2,3},{3,2},{4,5},{5,4},{6,7},{7,6},{8,9},{9,8},{10,11... | collective-permute-start | bytes 393224 | tf_op jit(solution)/shard_map/ppermute | solution.py:263
  22.5 8.1 %collective-permute-start.8 = (bf16[64,512]{1,0:T(8,128)(2,1)S(1)}, bf16[64,512]{1,0:T(8,128)(2,1)S(1)}, u32[]{:S(2)}, u32[]{:S(2)}) collective-permute-start(bf16[64,512]{1,0:T(8,128)(2,1)S(1)} %get-tuple-element.23), channel_id=1, source_target_pairs={{0,8},{8,0},{16,24},{24,16},{1,9},{9,1},{17,25},{25,17},{2,10},{10... | collective-permute-start | bytes 196616 | tf_op jit(solution)/shard_map/ppermute | solution.py:263
  24.1 8.9 %collective-permute-start.9 = (bf16[64,512]{1,0:T(8,128)(2,1)S(1)}, bf16[64,512]{1,0:T(8,128)(2,1)S(1)}, u32[]{:S(2)}, u32[]{:S(2)}) collective-permute-start(bf16[64,512]{1,0:T(8,128)(2,1)S(1)} %get-tuple-element.24), channel_id=1, source_target_pairs={{0,16},{8,24},{16,0},{24,8},{1,17},{9,25},{17,1},{25,9},{2,18},{10... | collective-permute-start | bytes 196616 | tf_op jit(solution)/shard_map/ppermute | solution.py:263
  26.7 6.4 %collective-permute-start.10 = (bf16[64,512]{1,0:T(8,128)(2,1)S(1)}, bf16[64,512]{1,0:T(8,128)(2,1)S(1)}, u32[]{:S(2)}, u32[]{:S(2)}) collective-permute-start(bf16[64,512]{1,0:T(8,128)(2,1)S(1)} %get-tuple-element.25), channel_id=1, source_target_pairs={{0,24},{8,16},{16,8},{24,0},{1,25},{9,17},{17,9},{25,1},{2,26},{10... | collective-permute-start | bytes 196616 | tf_op jit(solution)/shard_map/ppermute | solution.py:263
  26.9 8.9 %collective-permute-start.7 = (bf16[64,128]{1,0:T(8,128)(2,1)S(1)}, bf16[64,128]{1,0:T(8,128)(2,1)S(1)}, u32[]{:S(2)}, u32[]{:S(2)}) collective-permute-start(bf16[64,128]{1,0:T(8,128)(2,1)S(1)} %get-tuple-element.21.rest_0_), channel_id=1, source_target_pairs={{0,24},{8,16},{16,8},{24,0},{1,25},{9,17},{17,9},{25,1},{2,26},{10... | collective-permute-start | bytes 49160 | tf_op jit(solution)/shard_map/ppermute | solution.py:263
  30.5 6.2 %collective-permute-start.6 = (bf16[64,128]{1,0:T(8,128)(2,1)S(1)}, bf16[64,128]{1,0:T(8,128)(2,1)S(1)}, u32[]{:S(2)}, u32[]{:S(2)}) collective-permute-start(bf16[64,128]{1,0:T(8,128)(2,1)S(1)} %get-tuple-element.21.rest_0_), channel_id=1, source_target_pairs={{0,16},{8,24},{16,0},{24,8},{1,17},{9,25},{17,1},{25,9},{2,18},{10... | collective-permute-start | bytes 49160 | tf_op jit(solution)/shard_map/ppermute | solution.py:263
  33.0 4.6 %collective-permute-start.5 = (bf16[64,128]{1,0:T(8,128)(2,1)S(1)}, bf16[64,128]{1,0:T(8,128)(2,1)S(1)}, u32[]{:S(2)}, u32[]{:S(2)}) collective-permute-start(bf16[64,128]{1,0:T(8,128)(2,1)S(1)} %get-tuple-element.21.rest_0_), channel_id=1, source_target_pairs={{0,8},{8,0},{16,24},{24,16},{1,9},{9,1},{17,25},{25,17},{2,10},{10... | collective-permute-start | bytes 49160 | tf_op jit(solution)/shard_map/ppermute | solution.py:263
  33.0 9.1 %slice-start = ((s8[8388608]{0:T(1024)(128)(4,1)}), s8[4194304]{0:T(1024)(128)(4,1)S(1)}, s32[]{:S(2)}) async-start(s8[8388608]{0:T(1024)(128)(4,1)} %bitcast.4), calls=%async_computation | async-start | bytes 8388608
  33.1 9.1 %slice-start.1 = ((s8[8388608]{0:T(1024)(128)(4,1)}), s8[4194304]{0:T(1024)(128)(4,1)S(1)}, s32[]{:S(2)}) async-start(s8[8388608]{0:T(1024)(128)(4,1)} %bitcast.4), calls=%async_computation.1 | async-start | bytes 8388608
  33.1 9.0 %copy-start = (bf16[2048,64]{0,1:T(8,128)(2,1)S(1)}, bf16[2048,64]{0,1:T(8,128)(2,1)}, u32[]{:S(2)}) copy-start(bf16[2048,64]{0,1:T(8,128)(2,1)} %param.4) | copy-start | bytes 786436
  33.1 9.0 %copy-start.1 = (bf16[2048,64]{0,1:T(8,128)(2,1)S(1)}, bf16[2048,64]{0,1:T(8,128)(2,1)}, u32[]{:S(2)}) copy-start(bf16[2048,64]{0,1:T(8,128)(2,1)} %param.5) | copy-start | bytes 786436
  33.1 9.0 %collective-permute-start.13 = (bf16[64,512]{1,0:T(8,128)(2,1)S(1)}, bf16[64,512]{1,0:T(8,128)(2,1)S(1)}, u32[]{:S(2)}, u32[]{:S(2)}) collective-permute-start(bf16[64,512]{1,0:T(8,128)(2,1)S(1)} %shard_map.54.rest_0_), channel_id=1, source_target_pairs={{0,24},{8,16},{16,8},{24,0},{1,25},{9,17},{17,9},{25,1},{2,26},{10... | collective-permute-start | bytes 196616 | tf_op jit(solution)/shard_map/ppermute | solution.py:263
  35.8 6.4 %collective-permute-start.12 = (bf16[64,512]{1,0:T(8,128)(2,1)S(1)}, bf16[64,512]{1,0:T(8,128)(2,1)S(1)}, u32[]{:S(2)}, u32[]{:S(2)}) collective-permute-start(bf16[64,512]{1,0:T(8,128)(2,1)S(1)} %shard_map.54.rest_0_), channel_id=1, source_target_pairs={{0,16},{8,24},{16,0},{24,8},{1,17},{9,25},{17,1},{25,9},{2,18},{10... | collective-permute-start | bytes 196616 | tf_op jit(solution)/shard_map/ppermute | solution.py:263
  36.7 5.4 %collective-permute-start.11 = (bf16[64,512]{1,0:T(8,128)(2,1)S(1)}, bf16[64,512]{1,0:T(8,128)(2,1)S(1)}, u32[]{:S(2)}, u32[]{:S(2)}) collective-permute-start(bf16[64,512]{1,0:T(8,128)(2,1)S(1)} %shard_map.54.rest_0_), channel_id=1, source_target_pairs={{0,8},{8,0},{16,24},{24,16},{1,9},{9,1},{17,25},{25,17},{2,10},{10... | collective-permute-start | bytes 196616 | tf_op jit(solution)/shard_map/ppermute | solution.py:263
  49.1 1.4 %collective-permute-start.14 = (bf16[64,1152]{1,0:T(8,128)(2,1)S(1)}, bf16[64,1152]{1,0:T(8,128)(2,1)S(1)}, u32[]{:S(2)}, u32[]{:S(2)}) collective-permute-start(bf16[64,1152]{1,0:T(8,128)(2,1)S(1)} %get-tuple-element.27), channel_id=1, source_target_pairs={{0,1},{1,0},{2,3},{3,2},{4,5},{5,4},{6,7},{7,6},{8,9},{9,8},{10,11... | collective-permute-start | bytes 442376 | tf_op jit(solution)/shard_map/ppermute | solution.py:263
  50.7 7.7 %collective-permute-start.17 = (bf16[64,1152]{1,0:T(8,128)(2,1)S(1)}, bf16[64,1152]{1,0:T(8,128)(2,1)S(1)}, u32[]{:S(2)}, u32[]{:S(2)}) collective-permute-start(bf16[64,1152]{1,0:T(8,128)(2,1)S(1)} %shard_map.56.refs_0_), channel_id=1, source_target_pairs={{0,6},{1,7},{2,4},{3,5},{4,2},{5,3},{6,0},{7,1},{8,14},{9,15},{10,... | collective-permute-start | bytes 442376 | tf_op jit(solution)/shard_map/ppermute | solution.py:263
  52.4 8.3 %collective-permute-start.16 = (bf16[64,1152]{1,0:T(8,128)(2,1)S(1)}, bf16[64,1152]{1,0:T(8,128)(2,1)S(1)}, u32[]{:S(2)}, u32[]{:S(2)}) collective-permute-start(bf16[64,1152]{1,0:T(8,128)(2,1)S(1)} %shard_map.56.refs_0_), channel_id=1, source_target_pairs={{0,4},{1,5},{2,6},{3,7},{4,0},{5,1},{6,2},{7,3},{8,12},{9,13},{10,... | collective-permute-start | bytes 442376 | tf_op jit(solution)/shard_map/ppermute | solution.py:263
  53.7 7.0 %collective-permute-start.15 = (bf16[64,1152]{1,0:T(8,128)(2,1)S(1)}, bf16[64,1152]{1,0:T(8,128)(2,1)S(1)}, u32[]{:S(2)}, u32[]{:S(2)}) collective-permute-start(bf16[64,1152]{1,0:T(8,128)(2,1)S(1)} %shard_map.56.refs_0_), channel_id=1, source_target_pairs={{0,2},{1,3},{2,0},{3,1},{4,6},{5,7},{6,4},{7,5},{8,10},{9,11},{10,... | collective-permute-start | bytes 442376 | tf_op jit(solution)/shard_map/ppermute | solution.py:263
  61.0 14.6 %collective-permute-start.18 = (bf16[64,1024]{1,0:T(8,128)(2,1)S(1)}, bf16[64,1024]{1,0:T(8,128)(2,1)S(1)}, u32[]{:S(2)}, u32[]{:S(2)}) collective-permute-start(bf16[64,1024]{1,0:T(8,128)(2,1)S(1)} %get-tuple-element.28.own_half_ref), channel_id=1, source_target_pairs={{0,1},{1,0},{2,3},{3,2},{4,5},{5,4},{6,7},{7,6},{8,9},{9,8},{10,11... | collective-permute-start | bytes 393224 | tf_op jit(solution)/shard_map/ppermute | solution.py:263
  61.0 7.0 %collective-permute-start.22 = (bf16[64,512]{1,0:T(8,128)(2,1)S(1)}, bf16[64,512]{1,0:T(8,128)(2,1)S(1)}, u32[]{:S(2)}, u32[]{:S(2)}) collective-permute-start(bf16[64,512]{1,0:T(8,128)(2,1)S(1)} %get-tuple-element.31), channel_id=1, source_target_pairs={{0,8},{8,0},{16,24},{24,16},{1,9},{9,1},{17,25},{25,17},{2,10},{10... | collective-permute-start | bytes 196616 | tf_op jit(solution)/shard_map/ppermute | solution.py:263
  62.2 8.9 %collective-permute-start.23 = (bf16[64,512]{1,0:T(8,128)(2,1)S(1)}, bf16[64,512]{1,0:T(8,128)(2,1)S(1)}, u32[]{:S(2)}, u32[]{:S(2)}) collective-permute-start(bf16[64,512]{1,0:T(8,128)(2,1)S(1)} %get-tuple-element.32), channel_id=1, source_target_pairs={{0,16},{8,24},{16,0},{24,8},{1,17},{9,25},{17,1},{25,9},{2,18},{10... | collective-permute-start | bytes 196616 | tf_op jit(solution)/shard_map/ppermute | solution.py:263
  64.2 6.9 %collective-permute-start.24 = (bf16[64,512]{1,0:T(8,128)(2,1)S(1)}, bf16[64,512]{1,0:T(8,128)(2,1)S(1)}, u32[]{:S(2)}, u32[]{:S(2)}) collective-permute-start(bf16[64,512]{1,0:T(8,128)(2,1)S(1)} %get-tuple-element.33), channel_id=1, source_target_pairs={{0,24},{8,16},{16,8},{24,0},{1,25},{9,17},{17,9},{25,1},{2,26},{10... | collective-permute-start | bytes 196616 | tf_op jit(solution)/shard_map/ppermute | solution.py:263
  65.4 8.1 %collective-permute-start.21 = (bf16[64,128]{1,0:T(8,128)(2,1)S(1)}, bf16[64,128]{1,0:T(8,128)(2,1)S(1)}, u32[]{:S(2)}, u32[]{:S(2)}) collective-permute-start(bf16[64,128]{1,0:T(8,128)(2,1)S(1)} %get-tuple-element.29.rest_0_), channel_id=1, source_target_pairs={{0,24},{8,16},{16,8},{24,0},{1,25},{9,17},{17,9},{25,1},{2,26},{10... | collective-permute-start | bytes 49160 | tf_op jit(solution)/shard_map/ppermute | solution.py:263
  68.0 6.7 %collective-permute-start.20 = (bf16[64,128]{1,0:T(8,128)(2,1)S(1)}, bf16[64,128]{1,0:T(8,128)(2,1)S(1)}, u32[]{:S(2)}, u32[]{:S(2)}) collective-permute-start(bf16[64,128]{1,0:T(8,128)(2,1)S(1)} %get-tuple-element.29.rest_0_), channel_id=1, source_target_pairs={{0,16},{8,24},{16,0},{24,8},{1,17},{9,25},{17,1},{25,9},{2,18},{10... | collective-permute-start | bytes 49160 | tf_op jit(solution)/shard_map/ppermute | solution.py:263
  71.1 4.5 %collective-permute-start.19 = (bf16[64,128]{1,0:T(8,128)(2,1)S(1)}, bf16[64,128]{1,0:T(8,128)(2,1)S(1)}, u32[]{:S(2)}, u32[]{:S(2)}) collective-permute-start(bf16[64,128]{1,0:T(8,128)(2,1)S(1)} %get-tuple-element.29.rest_0_), channel_id=1, source_target_pairs={{0,8},{8,0},{16,24},{24,16},{1,9},{9,1},{17,25},{25,17},{2,10},{10... | collective-permute-start | bytes 49160 | tf_op jit(solution)/shard_map/ppermute | solution.py:263
  71.1 9.0 %collective-permute-start.27 = (bf16[64,512]{1,0:T(8,128)(2,1)S(1)}, bf16[64,512]{1,0:T(8,128)(2,1)S(1)}, u32[]{:S(2)}, u32[]{:S(2)}) collective-permute-start(bf16[64,512]{1,0:T(8,128)(2,1)S(1)} %shard_map.59.rest_0_), channel_id=1, source_target_pairs={{0,24},{8,16},{16,8},{24,0},{1,25},{9,17},{17,9},{25,1},{2,26},{10... | collective-permute-start | bytes 196616 | tf_op jit(solution)/shard_map/ppermute | solution.py:263
  73.5 6.6 %collective-permute-start.26 = (bf16[64,512]{1,0:T(8,128)(2,1)S(1)}, bf16[64,512]{1,0:T(8,128)(2,1)S(1)}, u32[]{:S(2)}, u32[]{:S(2)}) collective-permute-start(bf16[64,512]{1,0:T(8,128)(2,1)S(1)} %shard_map.59.rest_0_), channel_id=1, source_target_pairs={{0,16},{8,24},{16,0},{24,8},{1,17},{9,25},{17,1},{25,9},{2,18},{10... | collective-permute-start | bytes 196616 | tf_op jit(solution)/shard_map/ppermute | solution.py:263
  74.7 5.4 %collective-permute-start.25 = (bf16[64,512]{1,0:T(8,128)(2,1)S(1)}, bf16[64,512]{1,0:T(8,128)(2,1)S(1)}, u32[]{:S(2)}, u32[]{:S(2)}) collective-permute-start(bf16[64,512]{1,0:T(8,128)(2,1)S(1)} %shard_map.59.rest_0_), channel_id=1, source_target_pairs={{0,8},{8,0},{16,24},{24,16},{1,9},{9,1},{17,25},{25,17},{2,10},{10... | collective-permute-start | bytes 196616 | tf_op jit(solution)/shard_map/ppermute | solution.py:263

commit v2 on v1

--- a/solution.py
+++ b/solution.py
@@ -61,22 +61,27 @@
         y2_refs[k][...] = part.astype(y2_refs[k].dtype)
 
 
-def first_kernel(where_ref, movie_ref, vpt_ref, fpt_ref, own_ref, send_ref, *rest):
-    *y2_refs, y1_scr, y2_scr = rest
-    step = pl.program_id(0)
-    rows = movie_ref.shape[0]
-
-    @pl.when(step == 0)
-    def _():
-        y2_scr[...] = jnp.zeros_like(y2_scr)
-
-    cur = movie_ref[...]
-    y2_scr[...] += dot(fpt_ref[...], cur)
-    y1_scr[:, pl.ds(pl.multiple_of(step * rows, rows), rows)] = dot(vpt_ref[...], cur, ((1,), (1,)))
-
-    @pl.when(step == pl.num_programs(0) - 1)
-    def _():
-        finish_sketch(where_ref, y1_scr, y2_scr, vpt_ref, own_ref, send_ref, y2_refs)
+def first_kernel(blocks, where_ref, movie_ref, vpt_hbm, fpt_hbm, own_ref, send_ref, *rest):
+    *y2_refs, held, vpt_ref, fpt_ref, y1_scr, y2_scr, sems = rest
+    spans = [slice(start, stop) for start, stop in zip(blocks, blocks[1:])]
+    copies = [
+        pltpu.make_async_copy(movie_ref.at[span, :], held.at[span, :], sems.at[i]) for i, span in enumerate(spans)
+    ]
+    probes = [
+        pltpu.make_async_copy(fpt_hbm, fpt_ref, sems.at[len(spans)]),
+        pltpu.make_async_copy(vpt_hbm, vpt_ref, sems.at[len(spans) + 1]),
+    ]
+    for copy in [copies[0], *probes, *copies[1:]]:
+        copy.start()
+    for copy in probes:
+        copy.wait()
+    for i, span in enumerate(spans):
+        copies[i].wait()
+        cur = held[span, :]
+        part = dot(fpt_ref[:, span], cur)
+        y2_scr[...] = part if i == 0 else y2_scr[...] + part
+        y1_scr[:, span] = dot(vpt_ref[...], cur, ((1,), (1,)))
+    finish_sketch(where_ref, y1_scr, y2_scr, vpt_ref, own_ref, send_ref, y2_refs)
 
 
 def pair_kernel(own_ref, got_ref, msg_ref):
@@ -211,31 +216,28 @@
         finish_sketch(where_ref, y1_scr, y2_scr, vpt_ref, own_ref, send_ref, y2_refs)
 
 
-def last_kernel(n_row, chunk, where_ref, movie_ref, left_ref, *rest):
+def last_kernel(n_row, chunk, blocks, where_ref, movie_ref, left_ref, *rest):
     right_refs = rest[:n_row]
-    low_ref, sparse_ref, right_scr = rest[n_row:]
-    step = pl.program_id(0)
-    rows, voxels = low_ref.shape
-
-    @pl.when(step == 0)
-    def _():
-        join_right(where_ref, right_refs, right_scr)
-
-    span = pl.ds(pl.multiple_of(step * rows, rows), rows)
-    left = left_ref[span, :]
+    low_ref, sparse_ref, right_scr, low_scr, sparse_scr, sems = rest[n_row:]
+    voxels = low_scr.shape[1]
+    join_right(where_ref, right_refs, right_scr)
     cols = [slice(j, j + chunk) for j in range(0, voxels, chunk)]
-    ahead = dot(left, right_scr[:, cols[0]])
-    for j, c in enumerate(cols):
-        low = ahead
-        if j + 1 < len(cols):
-            ahead = dot(left, right_scr[:, cols[j + 1]])
-        low_ref[:, c] = low.astype(BF16)
-        gap = movie_ref[span, c].astype(F32) - low
-        sparse_ref[:, c] = (gap - jnp.clip(gap, -cutoff, cutoff)).astype(BF16)
-
-
-def block_rows(rows, width):
-    return pl.BlockSpec((rows, width), lambda i, *_: (i, 0))
+    copies = []
+    for i, span in enumerate(slice(start, stop) for start, stop in zip(blocks, blocks[1:])):
+        left = left_ref[span, :]
+        ahead = dot(left, right_scr[:, cols[0]])
+        for j, c in enumerate(cols):
+            low = ahead
+            if j + 1 < len(cols):
+                ahead = dot(left, right_scr[:, cols[j + 1]])
+            low_scr[span, c] = low.astype(BF16)
+            gap = movie_ref[span, c].astype(F32) - low
+            sparse_scr[span, c] = (gap - jnp.clip(gap, -cutoff, cutoff)).astype(BF16)
+        for k, (scr, ref) in enumerate(((low_scr, low_ref), (sparse_scr, sparse_ref))):
+            copies.append(pltpu.make_async_copy(scr.at[span, :], ref.at[span, :], sems.at[i, k]))
+            copies[-1].start()
+    for copy in copies:
+        copy.wait()
 
 
 def block_cols(rank, rows):
@@ -271,7 +273,6 @@
     width = half + 2 * rank
     rows = min(512, frames)
     mid_rows = min(1024, frames)
-    last_rows = min(512, frames)
     chunk = min(256, voxels)
     where = jnp.stack([lax.axis_index("vox") % 2, lax.axis_index("frm")]).astype(jnp.int32)
     vpt, fpt = voxel_probe.T, frame_probe.T
@@ -330,13 +331,14 @@
         )
         return [left, *rights]
 
+    blocks = [0, *range(rows // 2, frames, rows), frames]
     sketch = run(
-        first_kernel,
-        frames // rows,
-        [block_rows(rows, voxels), pl.BlockSpec((rank, voxels), lambda i, *_: (0, 0)), block_cols(rank, rows)],
+        functools.partial(first_kernel, blocks),
+        1,
+        [pl.BlockSpec(memory_space=pltpu.HBM)] * 3,
         sketch_specs,
         sketch_shapes,
-        sums,
+        [pltpu.VMEM(x.shape, BF16) for x in (movie, vpt, fpt)] + sums + [pltpu.SemaphoreType.DMA((len(blocks) + 1,))],
         2,
         tuple(pltpu.with_memory_space_constraint(x, pltpu.HBM) for x in (movie, vpt, fpt)),
         limit=44 * 1024 * 1024,
@@ -355,16 +357,19 @@
         )
         sides = share_sketch(*sketch)
     out = jax.ShapeDtypeStruct((frames, voxels), BF16)
+    starts = [*range(0, frames, rows // 2), frames]
     return tuple(
         run(
-            functools.partial(last_kernel, n_row, 256),
-            frames // last_rows,
+            functools.partial(last_kernel, n_row, chunk, starts),
+            1,
             [resident] + side_specs,
-            [block_rows(last_rows, voxels)] * 2,
+            [pl.BlockSpec(memory_space=pltpu.HBM)] * 2,
             [out, out],
-            [right],
+            [right, pltpu.VMEM(out.shape, BF16), pltpu.VMEM(out.shape, BF16)]
+            + [pltpu.SemaphoreType.DMA((len(starts) - 1, 2))],
             1,
             (movie, *sides),
+            limit=32 * 1024 * 1024,
         )
     )
 

time: 87.9 us -> 86.3 us (0.982)
  Pallas kernels: 32.8 us -> 31 us
    pallas_call x3, Pallas kernels: 22.9 us -> 21.1 us  [run(): pl.pallas_call(kernel, grid_spec=pltpu.PrefetchScalarGridSpec(num_scalar_...]
  transfers between devices with their start and end apart: 28 -> 28, of which waited for: 10 -> 10; matrix products, arithmetic and copies ran while one was open for 0% -> 0% of each run, Pallas kernels for 10% -> 11%
where the time goes in v2:
time: 86.3 us; the launch traced here: 86.2 us
  starting transfers between devices  32.8 us (38%)
  Pallas kernels  31 us (36%)
  waiting for transfers between devices  21.3 us (25%)
  between operations  0.98 us (1%)
    ppermute x28, starting transfers between devices, exchange(): return lax.ppermute(x, axis, [(i, i ^ k) for i in range(size)])  32.8 us
    ppermute x28, waiting for transfers between devices, exchange(): return lax.ppermute(x, axis, [(i, i ^ k) for i in range(size)])  21.3 us
    pallas_call x3, Pallas kernels, run(): pl.pallas_call(kernel, grid_spec=pltpu.PrefetchScalarGridSpec(num_scalar_...  21.1 us
    pallas_call x8, Pallas kernels, vmem_call(): pl.pallas_call(kernel, out_shape=outs, in_specs=([] if where is None else...  9.87 us
  transfers between devices with their start and end apart: 28, of which 10 were waited for; matrix products, arithmetic and copies ran while one was open for 0% of the time, Pallas kernels for 11%

profile of v2, /device:TPU:0, one launch (start us, length us, event | category | flops | bytes accessed | tf_op | source)
XLA Modules:
  0.0 86.2 jit_solution(13976791095413752496)
XLA Ops:
  0.7 6.9 %shard_map.50 = (f32[64,1152]{1,0:T(8,128)S(1)}, bf16[64,1152]{1,0:T(8,128)(2,1)S(1)}, f32[64,512]{1,0:T(8,128)S(1)}, bf16[64,512]{1,0:T(8,128)(2,1)S(1)}, bf16[...) custom-call(s32[2]{0:T(128)S(1)} %pad_add_fusion.where_ref, bf16[2048,2048]{1,0:T(8,128)(2,1)} %movie_ref.5, ...), custom_call_target="tpu_custom_call" | custom-call | flops 1073741824 | bytes 8388608 | tf_op jit(solution)/shard_map/pallas_call | solution.py:293
  7.7 0.6 collective-permute-start
  8.2 1.0 %collective-permute-done.got_ref = bf16[64,1152]{1,0:T(8,128)(2,1)S(1)} collective-permute-done((bf16[64,1152]{1,0:T(8,128)(2,1)S(1)}, bf16[64,1152]{1,0:T(8,128)(2,1)S(1)}, u32[]{:S(2)}, u32[]{:S(2)}) %collective-permute-start) | collective-permute-done | bytes 147488 | tf_op jit(solution)/shard_map/ppermute | solution.py:265
  9.4 3.8 %collective-permute-start.3 = (bf16[64,1152]{1,0:T(8,128)(2,1)S(1)}, bf16[64,1152]{1,0:T(8,128)(2,1)S(1)}, u32[]{:S(2)}, u32[]{:S(2)}) collective-permute-start(bf16[64,1152]{1,0:T(8,128)(2,1)S(1)} %shard_map.51.refs_0_), channel_id=1, source_target_pairs={{0,6},{1,7},{2,4},{3,5},{4,2},{5,3},{6,0},{7,1},{8,14},{9,15},{10,... | collective-permute-start | bytes 442376 | tf_op jit(solution)/shard_map/ppermute | solution.py:265
  13.2 0.5 collective-permute-start.2
  13.8 4.0 %collective-permute-done.3.refs_3_ = bf16[64,1152]{1,0:T(8,128)(2,1)S(1)} collective-permute-done((bf16[64,1152]{1,0:T(8,128)(2,1)S(1)}, bf16[64,1152]{1,0:T(8,128)(2,1)S(1)}, u32[]{:S(2)}, u32[]{:S(2)}) %collective-permute-start.3) | collective-permute-done | bytes 147488 | tf_op jit(solution)/shard_map/ppermute | solution.py:265
  17.9 2.6 %collective-permute-done.2.refs_2_ = bf16[64,1152]{1,0:T(8,128)(2,1)S(1)} collective-permute-done((bf16[64,1152]{1,0:T(8,128)(2,1)S(1)}, bf16[64,1152]{1,0:T(8,128)(2,1)S(1)}, u32[]{:S(2)}, u32[]{:S(2)}) %collective-permute-start.2) | collective-permute-done | bytes 147488 | tf_op jit(solution)/shard_map/ppermute | solution.py:265
  21.1 1.6 %collective-permute-start.8 = (bf16[64,512]{1,0:T(8,128)(2,1)S(1)}, bf16[64,512]{1,0:T(8,128)(2,1)S(1)}, u32[]{:S(2)}, u32[]{:S(2)}) collective-permute-start(bf16[64,512]{1,0:T(8,128)(2,1)S(1)} %get-tuple-element.23), channel_id=1, source_target_pairs={{0,8},{8,0},{16,24},{24,16},{1,9},{9,1},{17,25},{25,17},{2,10},{10... | collective-permute-start | bytes 196616 | tf_op jit(solution)/shard_map/ppermute | solution.py:265
  22.7 2.6 %collective-permute-start.9 = (bf16[64,512]{1,0:T(8,128)(2,1)S(1)}, bf16[64,512]{1,0:T(8,128)(2,1)S(1)}, u32[]{:S(2)}, u32[]{:S(2)}) collective-permute-start(bf16[64,512]{1,0:T(8,128)(2,1)S(1)} %get-tuple-element.24), channel_id=1, source_target_pairs={{0,16},{8,24},{16,0},{24,8},{1,17},{9,25},{17,1},{25,9},{2,18},{10... | collective-permute-start | bytes 196616 | tf_op jit(solution)/shard_map/ppermute | solution.py:265
  25.5 3.6 %collective-permute-start.7 = (bf16[64,128]{1,0:T(8,128)(2,1)S(1)}, bf16[64,128]{1,0:T(8,128)(2,1)S(1)}, u32[]{:S(2)}, u32[]{:S(2)}) collective-permute-start(bf16[64,128]{1,0:T(8,128)(2,1)S(1)} %get-tuple-element.21.rest_0_), channel_id=1, source_target_pairs={{0,24},{8,16},{16,8},{24,0},{1,25},{9,17},{17,9},{25,1},{2,26},{10... | collective-permute-start | bytes 49160 | tf_op jit(solution)/shard_map/ppermute | solution.py:265
  29.1 2.5 %collective-permute-done.9.refs_2_ = bf16[64,512]{1,0:T(8,128)(2,1)S(1)} collective-permute-done((bf16[64,512]{1,0:T(8,128)(2,1)S(1)}, bf16[64,512]{1,0:T(8,128)(2,1)S(1)}, u32[]{:S(2)}, u32[]{:S(2)}) %collective-permute-start.9) | collective-permute-done | bytes 65568 | tf_op jit(solution)/shard_map/ppermute | solution.py:265
  31.8 2.6 %collective-permute-start.13 = (bf16[64,512]{1,0:T(8,128)(2,1)S(1)}, bf16[64,512]{1,0:T(8,128)(2,1)S(1)}, u32[]{:S(2)}, u32[]{:S(2)}) collective-permute-start(bf16[64,512]{1,0:T(8,128)(2,1)S(1)} %shard_map.54.rest_0_), channel_id=1, source_target_pairs={{0,24},{8,16},{16,8},{24,0},{1,25},{9,17},{17,9},{25,1},{2,26},{10... | collective-permute-start | bytes 196616 | tf_op jit(solution)/shard_map/ppermute | solution.py:265
  34.4 0.9 %collective-permute-start.12 = (bf16[64,512]{1,0:T(8,128)(2,1)S(1)}, bf16[64,512]{1,0:T(8,128)(2,1)S(1)}, u32[]{:S(2)}, u32[]{:S(2)}) collective-permute-start(bf16[64,512]{1,0:T(8,128)(2,1)S(1)} %shard_map.54.rest_0_), channel_id=1, source_target_pairs={{0,16},{8,24},{16,0},{24,8},{1,17},{9,25},{17,1},{25,9},{2,18},{10... | collective-permute-start | bytes 196616 | tf_op jit(solution)/shard_map/ppermute | solution.py:265
  35.3 0.9 %collective-permute-start.11 = (bf16[64,512]{1,0:T(8,128)(2,1)S(1)}, bf16[64,512]{1,0:T(8,128)(2,1)S(1)}, u32[]{:S(2)}, u32[]{:S(2)}) collective-permute-start(bf16[64,512]{1,0:T(8,128)(2,1)S(1)} %shard_map.54.rest_0_), channel_id=1, source_target_pairs={{0,8},{8,0},{16,24},{24,16},{1,9},{9,1},{17,25},{25,17},{2,10},{10... | collective-permute-start | bytes 196616 | tf_op jit(solution)/shard_map/ppermute | solution.py:265
  36.2 4.5 %shard_map.53.left_ref = bf16[2048,64]{1,0:T(8,128)(2,1)S(1)} custom-call(s32[2]{0:T(128)S(1)} %pad_add_fusion.where_ref, bf16[64,1024]{1,0:T(8,128)(2,1)S(1)} %get-tuple-element.20.own_half_ref, bf16[64,1024]{1,0:T(8,128)(2,1)S(1)} %collective-permute-done.4.got_half_ref, bf16[64,128]{1,0:T(8,128)(2,1)S(1)} %get-tuple-element.21.rest_0_, ...), custom_call_target="tpu_custom_call" | custom-call | flops 5000000000 | bytes 589824 | tf_op jit(solution)/shard_map/pallas_call | solution.py:253
  40.8 7.1 %shard_map.55 = (f32[64,1152]{1,0:T(8,128)S(1)}, bf16[64,1152]{1,0:T(8,128)(2,1)S(1)}, f32[64,512]{1,0:T(8,128)S(1)}, bf16[64,512]{1,0:T(8,128)(2,1)S(1)}, bf16[...) custom-call(s32[2]{0:T(128)S(1)} %pad_add_fusion.where_ref, bf16[2048,2048]{1,0:T(8,128)(2,1)S(1)} %bitcast.5, ...), custom_call_target="tpu_custom_call" | custom-call | flops 1610612736 | bytes 8388608 | tf_op jit(solution)/shard_map/pallas_call | solution.py:293
  48.0 1.4 %collective-permute-done.14.got_ref = bf16[64,1152]{1,0:T(8,128)(2,1)S(1)} collective-permute-done((bf16[64,1152]{1,0:T(8,128)(2,1)S(1)}, bf16[64,1152]{1,0:T(8,128)(2,1)S(1)}, u32[]{:S(2)}, u32[]{:S(2)}) %collective-permute-start.14) | collective-permute-done | bytes 147488 | tf_op jit(solution)/shard_map/ppermute | solution.py:265
  49.5 1.7 %collective-permute-start.17 = (bf16[64,1152]{1,0:T(8,128)(2,1)S(1)}, bf16[64,1152]{1,0:T(8,128)(2,1)S(1)}, u32[]{:S(2)}, u32[]{:S(2)}) collective-permute-start(bf16[64,1152]{1,0:T(8,128)(2,1)S(1)} %shard_map.56.refs_0_), channel_id=1, source_target_pairs={{0,6},{1,7},{2,4},{3,5},{4,2},{5,3},{6,0},{7,1},{8,14},{9,15},{10,... | collective-permute-start | bytes 442376 | tf_op jit(solution)/shard_map/ppermute | solution.py:265
  51.2 1.3 %collective-permute-start.16 = (bf16[64,1152]{1,0:T(8,128)(2,1)S(1)}, bf16[64,1152]{1,0:T(8,128)(2,1)S(1)}, u32[]{:S(2)}, u32[]{:S(2)}) collective-permute-start(bf16[64,1152]{1,0:T(8,128)(2,1)S(1)} %shard_map.56.refs_0_), channel_id=1, source_target_pairs={{0,4},{1,5},{2,6},{3,7},{4,0},{5,1},{6,2},{7,3},{8,12},{9,13},{10,... | collective-permute-start | bytes 442376 | tf_op jit(solution)/shard_map/ppermute | solution.py:265
  52.5 0.5 collective-permute-start.15
  53.0 4.2 %collective-permute-done.17.refs_3_ = bf16[64,1152]{1,0:T(8,128)(2,1)S(1)} collective-permute-done((bf16[64,1152]{1,0:T(8,128)(2,1)S(1)}, bf16[64,1152]{1,0:T(8,128)(2,1)S(1)}, u32[]{:S(2)}, u32[]{:S(2)}) %collective-permute-start.17) | collective-permute-done | bytes 147488 | tf_op jit(solution)/shard_map/ppermute | solution.py:265
  57.2 2.3 %collective-permute-done.16.refs_2_ = bf16[64,1152]{1,0:T(8,128)(2,1)S(1)} collective-permute-done((bf16[64,1152]{1,0:T(8,128)(2,1)S(1)}, bf16[64,1152]{1,0:T(8,128)(2,1)S(1)}, u32[]{:S(2)}, u32[]{:S(2)}) %collective-permute-start.16) | collective-permute-done | bytes 147488 | tf_op jit(solution)/shard_map/ppermute | solution.py:265
  59.8 1.2 %collective-permute-start.22 = (bf16[64,512]{1,0:T(8,128)(2,1)S(1)}, bf16[64,512]{1,0:T(8,128)(2,1)S(1)}, u32[]{:S(2)}, u32[]{:S(2)}) collective-permute-start(bf16[64,512]{1,0:T(8,128)(2,1)S(1)} %get-tuple-element.31), channel_id=1, source_target_pairs={{0,8},{8,0},{16,24},{24,16},{1,9},{9,1},{17,25},{25,17},{2,10},{10... | collective-permute-start | bytes 196616 | tf_op jit(solution)/shard_map/ppermute | solution.py:265
  61.0 2.0 %collective-permute-start.23 = (bf16[64,512]{1,0:T(8,128)(2,1)S(1)}, bf16[64,512]{1,0:T(8,128)(2,1)S(1)}, u32[]{:S(2)}, u32[]{:S(2)}) collective-permute-start(bf16[64,512]{1,0:T(8,128)(2,1)S(1)} %get-tuple-element.32), channel_id=1, source_target_pairs={{0,16},{8,24},{16,0},{24,8},{1,17},{9,25},{17,1},{25,9},{2,18},{10... | collective-permute-start | bytes 196616 | tf_op jit(solution)/shard_map/ppermute | solution.py:265
  63.0 1.3 %collective-permute-start.24 = (bf16[64,512]{1,0:T(8,128)(2,1)S(1)}, bf16[64,512]{1,0:T(8,128)(2,1)S(1)}, u32[]{:S(2)}, u32[]{:S(2)}) collective-permute-start(bf16[64,512]{1,0:T(8,128)(2,1)S(1)} %get-tuple-element.33), channel_id=1, source_target_pairs={{0,24},{8,16},{16,8},{24,0},{1,25},{9,17},{17,9},{25,1},{2,26},{10... | collective-permute-start | bytes 196616 | tf_op jit(solution)/shard_map/ppermute | solution.py:265
  64.2 2.6 %collective-permute-start.21 = (bf16[64,128]{1,0:T(8,128)(2,1)S(1)}, bf16[64,128]{1,0:T(8,128)(2,1)S(1)}, u32[]{:S(2)}, u32[]{:S(2)}) collective-permute-start(bf16[64,128]{1,0:T(8,128)(2,1)S(1)} %get-tuple-element.29.rest_0_), channel_id=1, source_target_pairs={{0,24},{8,16},{16,8},{24,0},{1,25},{9,17},{17,9},{25,1},{2,26},{10... | collective-permute-start | bytes 49160 | tf_op jit(solution)/shard_map/ppermute | solution.py:265
  67.0 2.8 %collective-permute-done.23.refs_2_ = bf16[64,512]{1,0:T(8,128)(2,1)S(1)} collective-permute-done((bf16[64,512]{1,0:T(8,128)(2,1)S(1)}, bf16[64,512]{1,0:T(8,128)(2,1)S(1)}, u32[]{:S(2)}, u32[]{:S(2)}) %collective-permute-start.23) | collective-permute-done | bytes 65568 | tf_op jit(solution)/shard_map/ppermute | solution.py:265
  69.9 2.4 %collective-permute-start.27 = (bf16[64,512]{1,0:T(8,128)(2,1)S(1)}, bf16[64,512]{1,0:T(8,128)(2,1)S(1)}, u32[]{:S(2)}, u32[]{:S(2)}) collective-permute-start(bf16[64,512]{1,0:T(8,128)(2,1)S(1)} %shard_map.59.rest_0_), channel_id=1, source_target_pairs={{0,24},{8,16},{16,8},{24,0},{1,25},{9,17},{17,9},{25,1},{2,26},{10... | collective-permute-start | bytes 196616 | tf_op jit(solution)/shard_map/ppermute | solution.py:265
  72.3 1.2 %collective-permute-start.26 = (bf16[64,512]{1,0:T(8,128)(2,1)S(1)}, bf16[64,512]{1,0:T(8,128)(2,1)S(1)}, u32[]{:S(2)}, u32[]{:S(2)}) collective-permute-start(bf16[64,512]{1,0:T(8,128)(2,1)S(1)} %shard_map.59.rest_0_), channel_id=1, source_target_pairs={{0,16},{8,24},{16,0},{24,8},{1,17},{9,25},{17,1},{25,9},{2,18},{10... | collective-permute-start | bytes 196616 | tf_op jit(solution)/shard_map/ppermute | solution.py:265
  73.5 0.9 collective-permute-start.25
  74.4 4.5 %shard_map.58.left_ref = bf16[2048,64]{1,0:T(8,128)(2,1)S(1)} custom-call(s32[2]{0:T(128)S(1)} %pad_add_fusion.where_ref, bf16[64,1024]{1,0:T(8,128)(2,1)S(1)} %get-tuple-element.28.own_half_ref, bf16[64,1024]{1,0:T(8,128)(2,1)S(1)} %collective-permute-done.18.got_half_ref, bf16[64,128]{1,0:T(8,128)(2,1)S(1)} %get-tuple-element.29.rest_0_, ...), custom_call_target="tpu_custom_call" | custom-call | flops 5000000000 | bytes 589824 | tf_op jit(solution)/shard_map/pallas_call | solution.py:253
  79.0 7.0 %shard_map.60 = (bf16[2048,2048]{1,0:T(8,128)(2,1)}, bf16[2048,2048]{1,0:T(8,128)(2,1)}) custom-call(s32[2]{0:T(128)S(1)} %pad_add_fusion.where_ref, bf16[2048,2048]{1,0:T(8,128)(2,1)S(1)} %bitcast.5, bf16[2048,64]{1,0:T(8,128)(2,1)S(1)} %shard_map.58.left_ref, bf16[64,512]{1,0:T(8,128)(2,1)S(1)} %shard_map.59.rest_0_, ...), custom_call_target="tpu_custom_call" | custom-call | flops 536870912 | bytes 8388608 | tf_op jit(solution)/shard_map/pallas_call | solution.py:293
  (45 shorter events, 2.1 us)
Async XLA Ops:
  7.7 1.6 %collective-permute-start = (bf16[64,1152]{1,0:T(8,128)(2,1)S(1)}, bf16[64,1152]{1,0:T(8,128)(2,1)S(1)}, u32[]{:S(2)}, u32[]{:S(2)}) collective-permute-start(bf16[64,1152]{1,0:T(8,128)(2,1)S(1)} %get-tuple-element.19), channel_id=1, source_target_pairs={{0,1},{1,0},{2,3},{3,2},{4,5},{5,4},{6,7},{7,6},{8,9},{9,8},{10,11... | collective-permute-start | bytes 442376 | tf_op jit(solution)/shard_map/ppermute | solution.py:265
  9.4 8.5 %collective-permute-start.3 = (bf16[64,1152]{1,0:T(8,128)(2,1)S(1)}, bf16[64,1152]{1,0:T(8,128)(2,1)S(1)}, u32[]{:S(2)}, u32[]{:S(2)}) collective-permute-start(bf16[64,1152]{1,0:T(8,128)(2,1)S(1)} %shard_map.51.refs_0_), channel_id=1, source_target_pairs={{0,6},{1,7},{2,4},{3,5},{4,2},{5,3},{6,0},{7,1},{8,14},{9,15},{10,... | collective-permute-start | bytes 442376 | tf_op jit(solution)/shard_map/ppermute | solution.py:265
  13.2 7.3 %collective-permute-start.2 = (bf16[64,1152]{1,0:T(8,128)(2,1)S(1)}, bf16[64,1152]{1,0:T(8,128)(2,1)S(1)}, u32[]{:S(2)}, u32[]{:S(2)}) collective-permute-start(bf16[64,1152]{1,0:T(8,128)(2,1)S(1)} %shard_map.51.refs_0_), channel_id=1, source_target_pairs={{0,4},{1,5},{2,6},{3,7},{4,0},{5,1},{6,2},{7,3},{8,12},{9,13},{10,... | collective-permute-start | bytes 442376 | tf_op jit(solution)/shard_map/ppermute | solution.py:265
  13.7 7.1 %collective-permute-start.1 = (bf16[64,1152]{1,0:T(8,128)(2,1)S(1)}, bf16[64,1152]{1,0:T(8,128)(2,1)S(1)}, u32[]{:S(2)}, u32[]{:S(2)}) collective-permute-start(bf16[64,1152]{1,0:T(8,128)(2,1)S(1)} %shard_map.51.refs_0_), channel_id=1, source_target_pairs={{0,2},{1,3},{2,0},{3,1},{4,6},{5,7},{6,4},{7,5},{8,10},{9,11},{10,... | collective-permute-start | bytes 442376 | tf_op jit(solution)/shard_map/ppermute | solution.py:265
  21.1 15.2 %collective-permute-start.4 = (bf16[64,1024]{1,0:T(8,128)(2,1)S(1)}, bf16[64,1024]{1,0:T(8,128)(2,1)S(1)}, u32[]{:S(2)}, u32[]{:S(2)}) collective-permute-start(bf16[64,1024]{1,0:T(8,128)(2,1)S(1)} %get-tuple-element.20.own_half_ref), channel_id=1, source_target_pairs={{0,1},{1,0},{2,3},{3,2},{4,5},{5,4},{6,7},{7,6},{8,9},{9,8},{10,11... | collective-permute-start | bytes 393224 | tf_op jit(solution)/shard_map/ppermute | solution.py:265
  21.1 8.1 %collective-permute-start.8 = (bf16[64,512]{1,0:T(8,128)(2,1)S(1)}, bf16[64,512]{1,0:T(8,128)(2,1)S(1)}, u32[]{:S(2)}, u32[]{:S(2)}) collective-permute-start(bf16[64,512]{1,0:T(8,128)(2,1)S(1)} %get-tuple-element.23), channel_id=1, source_target_pairs={{0,8},{8,0},{16,24},{24,16},{1,9},{9,1},{17,25},{25,17},{2,10},{10... | collective-permute-start | bytes 196616 | tf_op jit(solution)/shard_map/ppermute | solution.py:265
  22.7 8.9 %collective-permute-start.9 = (bf16[64,512]{1,0:T(8,128)(2,1)S(1)}, bf16[64,512]{1,0:T(8,128)(2,1)S(1)}, u32[]{:S(2)}, u32[]{:S(2)}) collective-permute-start(bf16[64,512]{1,0:T(8,128)(2,1)S(1)} %get-tuple-element.24), channel_id=1, source_target_pairs={{0,16},{8,24},{16,0},{24,8},{1,17},{9,25},{17,1},{25,9},{2,18},{10... | collective-permute-start | bytes 196616 | tf_op jit(solution)/shard_map/ppermute | solution.py:265
  25.3 6.4 %collective-permute-start.10 = (bf16[64,512]{1,0:T(8,128)(2,1)S(1)}, bf16[64,512]{1,0:T(8,128)(2,1)S(1)}, u32[]{:S(2)}, u32[]{:S(2)}) collective-permute-start(bf16[64,512]{1,0:T(8,128)(2,1)S(1)} %get-tuple-element.25), channel_id=1, source_target_pairs={{0,24},{8,16},{16,8},{24,0},{1,25},{9,17},{17,9},{25,1},{2,26},{10... | collective-permute-start | bytes 196616 | tf_op jit(solution)/shard_map/ppermute | solution.py:265
  25.5 8.9 %collective-permute-start.7 = (bf16[64,128]{1,0:T(8,128)(2,1)S(1)}, bf16[64,128]{1,0:T(8,128)(2,1)S(1)}, u32[]{:S(2)}, u32[]{:S(2)}) collective-permute-start(bf16[64,128]{1,0:T(8,128)(2,1)S(1)} %get-tuple-element.21.rest_0_), channel_id=1, source_target_pairs={{0,24},{8,16},{16,8},{24,0},{1,25},{9,17},{17,9},{25,1},{2,26},{10... | collective-permute-start | bytes 49160 | tf_op jit(solution)/shard_map/ppermute | solution.py:265
  29.1 6.2 %collective-permute-start.6 = (bf16[64,128]{1,0:T(8,128)(2,1)S(1)}, bf16[64,128]{1,0:T(8,128)(2,1)S(1)}, u32[]{:S(2)}, u32[]{:S(2)}) collective-permute-start(bf16[64,128]{1,0:T(8,128)(2,1)S(1)} %get-tuple-element.21.rest_0_), channel_id=1, source_target_pairs={{0,16},{8,24},{16,0},{24,8},{1,17},{9,25},{17,1},{25,9},{2,18},{10... | collective-permute-start | bytes 49160 | tf_op jit(solution)/shard_map/ppermute | solution.py:265
  31.7 4.6 %collective-permute-start.5 = (bf16[64,128]{1,0:T(8,128)(2,1)S(1)}, bf16[64,128]{1,0:T(8,128)(2,1)S(1)}, u32[]{:S(2)}, u32[]{:S(2)}) collective-permute-start(bf16[64,128]{1,0:T(8,128)(2,1)S(1)} %get-tuple-element.21.rest_0_), channel_id=1, source_target_pairs={{0,8},{8,0},{16,24},{24,16},{1,9},{9,1},{17,25},{25,17},{2,10},{10... | collective-permute-start | bytes 49160 | tf_op jit(solution)/shard_map/ppermute | solution.py:265
  31.7 9.1 %slice-start = ((s8[8388608]{0:T(1024)(128)(4,1)}), s8[4194304]{0:T(1024)(128)(4,1)S(1)}, s32[]{:S(2)}) async-start(s8[8388608]{0:T(1024)(128)(4,1)} %bitcast.4), calls=%async_computation | async-start | bytes 8388608
  31.7 9.1 %slice-start.1 = ((s8[8388608]{0:T(1024)(128)(4,1)}), s8[4194304]{0:T(1024)(128)(4,1)S(1)}, s32[]{:S(2)}) async-start(s8[8388608]{0:T(1024)(128)(4,1)} %bitcast.4), calls=%async_computation.1 | async-start | bytes 8388608
  31.7 9.0 %copy-start = (bf16[2048,64]{0,1:T(8,128)(2,1)S(1)}, bf16[2048,64]{0,1:T(8,128)(2,1)}, u32[]{:S(2)}) copy-start(bf16[2048,64]{0,1:T(8,128)(2,1)} %param.4) | copy-start | bytes 786436
  31.7 9.0 %copy-start.1 = (bf16[2048,64]{0,1:T(8,128)(2,1)S(1)}, bf16[2048,64]{0,1:T(8,128)(2,1)}, u32[]{:S(2)}) copy-start(bf16[2048,64]{0,1:T(8,128)(2,1)} %param.5) | copy-start | bytes 786436
  31.8 9.0 %collective-permute-start.13 = (bf16[64,512]{1,0:T(8,128)(2,1)S(1)}, bf16[64,512]{1,0:T(8,128)(2,1)S(1)}, u32[]{:S(2)}, u32[]{:S(2)}) collective-permute-start(bf16[64,512]{1,0:T(8,128)(2,1)S(1)} %shard_map.54.rest_0_), channel_id=1, source_target_pairs={{0,24},{8,16},{16,8},{24,0},{1,25},{9,17},{17,9},{25,1},{2,26},{10... | collective-permute-start | bytes 196616 | tf_op jit(solution)/shard_map/ppermute | solution.py:265
  34.4 6.4 %collective-permute-start.12 = (bf16[64,512]{1,0:T(8,128)(2,1)S(1)}, bf16[64,512]{1,0:T(8,128)(2,1)S(1)}, u32[]{:S(2)}, u32[]{:S(2)}) collective-permute-start(bf16[64,512]{1,0:T(8,128)(2,1)S(1)} %shard_map.54.rest_0_), channel_id=1, source_target_pairs={{0,16},{8,24},{16,0},{24,8},{1,17},{9,25},{17,1},{25,9},{2,18},{10... | collective-permute-start | bytes 196616 | tf_op jit(solution)/shard_map/ppermute | solution.py:265
  35.3 5.4 %collective-permute-start.11 = (bf16[64,512]{1,0:T(8,128)(2,1)S(1)}, bf16[64,512]{1,0:T(8,128)(2,1)S(1)}, u32[]{:S(2)}, u32[]{:S(2)}) collective-permute-start(bf16[64,512]{1,0:T(8,128)(2,1)S(1)} %shard_map.54.rest_0_), channel_id=1, source_target_pairs={{0,8},{8,0},{16,24},{24,16},{1,9},{9,1},{17,25},{25,17},{2,10},{10... | collective-permute-start | bytes 196616 | tf_op jit(solution)/shard_map/ppermute | solution.py:265
  47.9 1.4 %collective-permute-start.14 = (bf16[64,1152]{1,0:T(8,128)(2,1)S(1)}, bf16[64,1152]{1,0:T(8,128)(2,1)S(1)}, u32[]{:S(2)}, u32[]{:S(2)}) collective-permute-start(bf16[64,1152]{1,0:T(8,128)(2,1)S(1)} %get-tuple-element.27), channel_id=1, source_target_pairs={{0,1},{1,0},{2,3},{3,2},{4,5},{5,4},{6,7},{7,6},{8,9},{9,8},{10,11... | collective-permute-start | bytes 442376 | tf_op jit(solution)/shard_map/ppermute | solution.py:265
  49.5 7.7 %collective-permute-start.17 = (bf16[64,1152]{1,0:T(8,128)(2,1)S(1)}, bf16[64,1152]{1,0:T(8,128)(2,1)S(1)}, u32[]{:S(2)}, u32[]{:S(2)}) collective-permute-start(bf16[64,1152]{1,0:T(8,128)(2,1)S(1)} %shard_map.56.refs_0_), channel_id=1, source_target_pairs={{0,6},{1,7},{2,4},{3,5},{4,2},{5,3},{6,0},{7,1},{8,14},{9,15},{10,... | collective-permute-start | bytes 442376 | tf_op jit(solution)/shard_map/ppermute | solution.py:265
  51.2 8.3 %collective-permute-start.16 = (bf16[64,1152]{1,0:T(8,128)(2,1)S(1)}, bf16[64,1152]{1,0:T(8,128)(2,1)S(1)}, u32[]{:S(2)}, u32[]{:S(2)}) collective-permute-start(bf16[64,1152]{1,0:T(8,128)(2,1)S(1)} %shard_map.56.refs_0_), channel_id=1, source_target_pairs={{0,4},{1,5},{2,6},{3,7},{4,0},{5,1},{6,2},{7,3},{8,12},{9,13},{10,... | collective-permute-start | bytes 442376 | tf_op jit(solution)/shard_map/ppermute | solution.py:265
  52.5 7.0 %collective-permute-start.15 = (bf16[64,1152]{1,0:T(8,128)(2,1)S(1)}, bf16[64,1152]{1,0:T(8,128)(2,1)S(1)}, u32[]{:S(2)}, u32[]{:S(2)}) collective-permute-start(bf16[64,1152]{1,0:T(8,128)(2,1)S(1)} %shard_map.56.refs_0_), channel_id=1, source_target_pairs={{0,2},{1,3},{2,0},{3,1},{4,6},{5,7},{6,4},{7,5},{8,10},{9,11},{10,... | collective-permute-start | bytes 442376 | tf_op jit(solution)/shard_map/ppermute | solution.py:265
  59.8 14.6 %collective-permute-start.18 = (bf16[64,1024]{1,0:T(8,128)(2,1)S(1)}, bf16[64,1024]{1,0:T(8,128)(2,1)S(1)}, u32[]{:S(2)}, u32[]{:S(2)}) collective-permute-start(bf16[64,1024]{1,0:T(8,128)(2,1)S(1)} %get-tuple-element.28.own_half_ref), channel_id=1, source_target_pairs={{0,1},{1,0},{2,3},{3,2},{4,5},{5,4},{6,7},{7,6},{8,9},{9,8},{10,11... | collective-permute-start | bytes 393224 | tf_op jit(solution)/shard_map/ppermute | solution.py:265
  59.8 7.0 %collective-permute-start.22 = (bf16[64,512]{1,0:T(8,128)(2,1)S(1)}, bf16[64,512]{1,0:T(8,128)(2,1)S(1)}, u32[]{:S(2)}, u32[]{:S(2)}) collective-permute-start(bf16[64,512]{1,0:T(8,128)(2,1)S(1)} %get-tuple-element.31), channel_id=1, source_target_pairs={{0,8},{8,0},{16,24},{24,16},{1,9},{9,1},{17,25},{25,17},{2,10},{10... | collective-permute-start | bytes 196616 | tf_op jit(solution)/shard_map/ppermute | solution.py:265
  61.0 8.9 %collective-permute-start.23 = (bf16[64,512]{1,0:T(8,128)(2,1)S(1)}, bf16[64,512]{1,0:T(8,128)(2,1)S(1)}, u32[]{:S(2)}, u32[]{:S(2)}) collective-permute-start(bf16[64,512]{1,0:T(8,128)(2,1)S(1)} %get-tuple-element.32), channel_id=1, source_target_pairs={{0,16},{8,24},{16,0},{24,8},{1,17},{9,25},{17,1},{25,9},{2,18},{10... | collective-permute-start | bytes 196616 | tf_op jit(solution)/shard_map/ppermute | solution.py:265
  63.0 6.9 %collective-permute-start.24 = (bf16[64,512]{1,0:T(8,128)(2,1)S(1)}, bf16[64,512]{1,0:T(8,128)(2,1)S(1)}, u32[]{:S(2)}, u32[]{:S(2)}) collective-permute-start(bf16[64,512]{1,0:T(8,128)(2,1)S(1)} %get-tuple-element.33), channel_id=1, source_target_pairs={{0,24},{8,16},{16,8},{24,0},{1,25},{9,17},{17,9},{25,1},{2,26},{10... | collective-permute-start | bytes 196616 | tf_op jit(solution)/shard_map/ppermute | solution.py:265
  64.2 8.1 %collective-permute-start.21 = (bf16[64,128]{1,0:T(8,128)(2,1)S(1)}, bf16[64,128]{1,0:T(8,128)(2,1)S(1)}, u32[]{:S(2)}, u32[]{:S(2)}) collective-permute-start(bf16[64,128]{1,0:T(8,128)(2,1)S(1)} %get-tuple-element.29.rest_0_), channel_id=1, source_target_pairs={{0,24},{8,16},{16,8},{24,0},{1,25},{9,17},{17,9},{25,1},{2,26},{10... | collective-permute-start | bytes 49160 | tf_op jit(solution)/shard_map/ppermute | solution.py:265
  66.8 6.7 %collective-permute-start.20 = (bf16[64,128]{1,0:T(8,128)(2,1)S(1)}, bf16[64,128]{1,0:T(8,128)(2,1)S(1)}, u32[]{:S(2)}, u32[]{:S(2)}) collective-permute-start(bf16[64,128]{1,0:T(8,128)(2,1)S(1)} %get-tuple-element.29.rest_0_), channel_id=1, source_target_pairs={{0,16},{8,24},{16,0},{24,8},{1,17},{9,25},{17,1},{25,9},{2,18},{10... | collective-permute-start | bytes 49160 | tf_op jit(solution)/shard_map/ppermute | solution.py:265
  69.9 4.5 %collective-permute-start.19 = (bf16[64,128]{1,0:T(8,128)(2,1)S(1)}, bf16[64,128]{1,0:T(8,128)(2,1)S(1)}, u32[]{:S(2)}, u32[]{:S(2)}) collective-permute-start(bf16[64,128]{1,0:T(8,128)(2,1)S(1)} %get-tuple-element.29.rest_0_), channel_id=1, source_target_pairs={{0,8},{8,0},{16,24},{24,16},{1,9},{9,1},{17,25},{25,17},{2,10},{10... | collective-permute-start | bytes 49160 | tf_op jit(solution)/shard_map/ppermute | solution.py:265
  69.9 9.0 %collective-permute-start.27 = (bf16[64,512]{1,0:T(8,128)(2,1)S(1)}, bf16[64,512]{1,0:T(8,128)(2,1)S(1)}, u32[]{:S(2)}, u32[]{:S(2)}) collective-permute-start(bf16[64,512]{1,0:T(8,128)(2,1)S(1)} %shard_map.59.rest_0_), channel_id=1, source_target_pairs={{0,24},{8,16},{16,8},{24,0},{1,25},{9,17},{17,9},{25,1},{2,26},{10... | collective-permute-start | bytes 196616 | tf_op jit(solution)/shard_map/ppermute | solution.py:265
  72.3 6.6 %collective-permute-start.26 = (bf16[64,512]{1,0:T(8,128)(2,1)S(1)}, bf16[64,512]{1,0:T(8,128)(2,1)S(1)}, u32[]{:S(2)}, u32[]{:S(2)}) collective-permute-start(bf16[64,512]{1,0:T(8,128)(2,1)S(1)} %shard_map.59.rest_0_), channel_id=1, source_target_pairs={{0,16},{8,24},{16,0},{24,8},{1,17},{9,25},{17,1},{25,9},{2,18},{10... | collective-permute-start | bytes 196616 | tf_op jit(solution)/shard_map/ppermute | solution.py:265
  73.5 5.4 %collective-permute-start.25 = (bf16[64,512]{1,0:T(8,128)(2,1)S(1)}, bf16[64,512]{1,0:T(8,128)(2,1)S(1)}, u32[]{:S(2)}, u32[]{:S(2)}) collective-permute-start(bf16[64,512]{1,0:T(8,128)(2,1)S(1)} %shard_map.59.rest_0_), channel_id=1, source_target_pairs={{0,8},{8,0},{16,24},{24,16},{1,9},{9,1},{17,25},{25,17},{2,10},{10... | collective-permute-start | bytes 196616 | tf_op jit(solution)/shard_map/ppermute | solution.py:265

commit v3 on v2

--- a/solution.py
+++ b/solution.py
@@ -120,8 +120,8 @@
     r = lax.broadcasted_iota(jnp.int32, (rank, rank), 0)
     c = lax.broadcasted_iota(jnp.int32, (rank, rank), 1)
     eye = (r == c).astype(F32)
-    shift = ridge_scale * (jnp.sum(gram * eye) / rank + 1e-06)
-    table = jnp.concatenate([gram + shift * eye, core.T], axis=1)
+    scale = 1.0 / (jnp.sum(gram * eye) / rank + 1e-06)
+    table = jnp.concatenate([gram * scale + ridge_scale * eye, core.T * scale], axis=1)
     width = table.shape[1]
     tall = 8
     tile = (tall, width)
@@ -135,17 +135,17 @@
         r0, r1, r2, r3 = [row(tiles[own], j) for j in range(4)]
         a, b, d = at(0, 0), at(1, 0), at(1, 1)
         e0, e1, f0, f1 = at(2, 0), at(2, 1), at(3, 0), at(3, 1)
-        inv = 1.0 / (a * d - b * b)
-        u0, u1 = (d * e0 - b * e1) * inv, (a * e1 - b * e0) * inv
-        v0, v1 = (d * f0 - b * f1) * inv, (a * f1 - b * f0) * inv
-        p = at(2, 2) - (e0 * u0 + e1 * u1)
-        q = at(3, 2) - (e0 * v0 + e1 * v1)
-        t = at(3, 3) - (f0 * v0 + f1 * v1)
-        inv_late = 1.0 / (p * t - q * q)
+        det = a * d - b * b
+        w0, w1, z0, z1 = d * e0 - b * e1, a * e1 - b * e0, d * f0 - b * f1, a * f1 - b * f0
+        p = at(2, 2) * det - (e0 * w0 + e1 * w1)
+        q = at(3, 2) * det - (e0 * z0 + e1 * z1)
+        t = at(3, 3) * det - (f0 * z0 + f1 * z1)
+        inv, inv_late = 1.0 / det, det * (1.0 / (p * t - q * q))
         n0, n1 = (r0 * d - r1 * b) * inv, (r1 * a - r0 * b) * inv
         s2, s3 = r2 - (e0 * n0 + e1 * n1), r3 - (f0 * n0 + f1 * n1)
         n2, n3 = (s2 * t - s3 * q) * inv_late, (s3 * p - s2 * q) * inv_late
-        n0, n1 = n0 - (u0 * n2 + v0 * n3), n1 - (u1 * n2 + v1 * n3)
+        n0 = n0 - (w0 * n2 + z0 * n3) * inv
+        n1 = n1 - (w1 * n2 + z1 * n3) * inv
         for j in range(4):
             cols[j][own] = cols[j][own] - (line == i + j).astype(F32)
         tiles = [
@@ -272,7 +272,7 @@
     half, share = frames // 2, voxels // n_row
     width = half + 2 * rank
     rows = min(512, frames)
-    mid_rows = min(1024, frames)
+    mid_rows = frames
     chunk = min(256, voxels)
     where = jnp.stack([lax.axis_index("vox") % 2, lax.axis_index("frm")]).astype(jnp.int32)
     vpt, fpt = voxel_probe.T, frame_probe.T

time: 86.3 us -> 86 us (level)
  transfers between devices with their start and end apart: 28 -> 28, of which waited for: 10 -> 9; matrix products, arithmetic and copies ran while one was open for 0% -> 0% of each run, Pallas kernels for 11% -> 11%
where the time goes in v3:
time: 86 us; the launch traced here: 85.8 us
  starting transfers between devices  32.8 us (38%)
  Pallas kernels  30.7 us (36%)
  waiting for transfers between devices  21.2 us (25%)
  between operations  0.99 us (1%)
    ppermute x28, starting transfers between devices, exchange(): return lax.ppermute(x, axis, [(i, i ^ k) for i in range(size)])  32.8 us
    ppermute x28, waiting for transfers between devices, exchange(): return lax.ppermute(x, axis, [(i, i ^ k) for i in range(size)])  21.2 us
    pallas_call x3, Pallas kernels, run(): pl.pallas_call(kernel, grid_spec=pltpu.PrefetchScalarGridSpec(num_scalar_...  20.8 us
    pallas_call x8, Pallas kernels, vmem_call(): pl.pallas_call(kernel, out_shape=outs, in_specs=([] if where is None else...  9.94 us
  transfers between devices with their start and end apart: 28, of which 9 were waited for; matrix products, arithmetic and copies ran while one was open for 0% of the time, Pallas kernels for 11%

profile of v3, /device:TPU:0, one launch (start us, length us, event | category | flops | bytes accessed | tf_op | source)
XLA Modules:
  0.0 85.8 jit_solution(8513664666550223617)
XLA Ops:
  0.7 6.9 %shard_map.50 = (f32[64,1152]{1,0:T(8,128)S(1)}, bf16[64,1152]{1,0:T(8,128)(2,1)S(1)}, f32[64,512]{1,0:T(8,128)S(1)}, bf16[64,512]{1,0:T(8,128)(2,1)S(1)}, bf16[...) custom-call(s32[2]{0:T(128)S(1)} %pad_add_fusion.where_ref, bf16[2048,2048]{1,0:T(8,128)(2,1)} %movie_ref.5, ...), custom_call_target="tpu_custom_call" | custom-call | flops 1073741824 | bytes 8388608 | tf_op jit(solution)/shard_map/pallas_call | solution.py:293
  7.7 0.6 collective-permute-start
  8.2 1.0 %collective-permute-done.got_ref = bf16[64,1152]{1,0:T(8,128)(2,1)S(1)} collective-permute-done((bf16[64,1152]{1,0:T(8,128)(2,1)S(1)}, bf16[64,1152]{1,0:T(8,128)(2,1)S(1)}, u32[]{:S(2)}, u32[]{:S(2)}) %collective-permute-start) | collective-permute-done | bytes 147488 | tf_op jit(solution)/shard_map/ppermute | solution.py:265
  9.4 3.8 %collective-permute-start.3 = (bf16[64,1152]{1,0:T(8,128)(2,1)S(1)}, bf16[64,1152]{1,0:T(8,128)(2,1)S(1)}, u32[]{:S(2)}, u32[]{:S(2)}) collective-permute-start(bf16[64,1152]{1,0:T(8,128)(2,1)S(1)} %shard_map.51.refs_0_), channel_id=1, source_target_pairs={{0,6},{1,7},{2,4},{3,5},{4,2},{5,3},{6,0},{7,1},{8,14},{9,15},{10,... | collective-permute-start | bytes 442376 | tf_op jit(solution)/shard_map/ppermute | solution.py:265
  13.2 0.5 collective-permute-start.2
  13.8 4.0 %collective-permute-done.3.refs_3_ = bf16[64,1152]{1,0:T(8,128)(2,1)S(1)} collective-permute-done((bf16[64,1152]{1,0:T(8,128)(2,1)S(1)}, bf16[64,1152]{1,0:T(8,128)(2,1)S(1)}, u32[]{:S(2)}, u32[]{:S(2)}) %collective-permute-start.3) | collective-permute-done | bytes 147488 | tf_op jit(solution)/shard_map/ppermute | solution.py:265
  17.9 2.6 %collective-permute-done.2.refs_2_ = bf16[64,1152]{1,0:T(8,128)(2,1)S(1)} collective-permute-done((bf16[64,1152]{1,0:T(8,128)(2,1)S(1)}, bf16[64,1152]{1,0:T(8,128)(2,1)S(1)}, u32[]{:S(2)}, u32[]{:S(2)}) %collective-permute-start.2) | collective-permute-done | bytes 147488 | tf_op jit(solution)/shard_map/ppermute | solution.py:265
  21.1 1.6 %collective-permute-start.8 = (bf16[64,512]{1,0:T(8,128)(2,1)S(1)}, bf16[64,512]{1,0:T(8,128)(2,1)S(1)}, u32[]{:S(2)}, u32[]{:S(2)}) collective-permute-start(bf16[64,512]{1,0:T(8,128)(2,1)S(1)} %get-tuple-element.23), channel_id=1, source_target_pairs={{0,8},{8,0},{16,24},{24,16},{1,9},{9,1},{17,25},{25,17},{2,10},{10... | collective-permute-start | bytes 196616 | tf_op jit(solution)/shard_map/ppermute | solution.py:265
  22.7 2.6 %collective-permute-start.9 = (bf16[64,512]{1,0:T(8,128)(2,1)S(1)}, bf16[64,512]{1,0:T(8,128)(2,1)S(1)}, u32[]{:S(2)}, u32[]{:S(2)}) collective-permute-start(bf16[64,512]{1,0:T(8,128)(2,1)S(1)} %get-tuple-element.24), channel_id=1, source_target_pairs={{0,16},{8,24},{16,0},{24,8},{1,17},{9,25},{17,1},{25,9},{2,18},{10... | collective-permute-start | bytes 196616 | tf_op jit(solution)/shard_map/ppermute | solution.py:265
  25.5 3.6 %collective-permute-start.7 = (bf16[64,128]{1,0:T(8,128)(2,1)S(1)}, bf16[64,128]{1,0:T(8,128)(2,1)S(1)}, u32[]{:S(2)}, u32[]{:S(2)}) collective-permute-start(bf16[64,128]{1,0:T(8,128)(2,1)S(1)} %get-tuple-element.21.rest_0_), channel_id=1, source_target_pairs={{0,24},{8,16},{16,8},{24,0},{1,25},{9,17},{17,9},{25,1},{2,26},{10... | collective-permute-start | bytes 49160 | tf_op jit(solution)/shard_map/ppermute | solution.py:265
  29.1 2.5 %collective-permute-done.9.refs_2_ = bf16[64,512]{1,0:T(8,128)(2,1)S(1)} collective-permute-done((bf16[64,512]{1,0:T(8,128)(2,1)S(1)}, bf16[64,512]{1,0:T(8,128)(2,1)S(1)}, u32[]{:S(2)}, u32[]{:S(2)}) %collective-permute-start.9) | collective-permute-done | bytes 65568 | tf_op jit(solution)/shard_map/ppermute | solution.py:265
  31.8 2.6 %collective-permute-start.13 = (bf16[64,512]{1,0:T(8,128)(2,1)S(1)}, bf16[64,512]{1,0:T(8,128)(2,1)S(1)}, u32[]{:S(2)}, u32[]{:S(2)}) collective-permute-start(bf16[64,512]{1,0:T(8,128)(2,1)S(1)} %shard_map.54.rest_0_), channel_id=1, source_target_pairs={{0,24},{8,16},{16,8},{24,0},{1,25},{9,17},{17,9},{25,1},{2,26},{10... | collective-permute-start | bytes 196616 | tf_op jit(solution)/shard_map/ppermute | solution.py:265
  34.4 0.9 %collective-permute-start.12 = (bf16[64,512]{1,0:T(8,128)(2,1)S(1)}, bf16[64,512]{1,0:T(8,128)(2,1)S(1)}, u32[]{:S(2)}, u32[]{:S(2)}) collective-permute-start(bf16[64,512]{1,0:T(8,128)(2,1)S(1)} %shard_map.54.rest_0_), channel_id=1, source_target_pairs={{0,16},{8,24},{16,0},{24,8},{1,17},{9,25},{17,1},{25,9},{2,18},{10... | collective-permute-start | bytes 196616 | tf_op jit(solution)/shard_map/ppermute | solution.py:265
  35.3 0.9 %collective-permute-start.11 = (bf16[64,512]{1,0:T(8,128)(2,1)S(1)}, bf16[64,512]{1,0:T(8,128)(2,1)S(1)}, u32[]{:S(2)}, u32[]{:S(2)}) collective-permute-start(bf16[64,512]{1,0:T(8,128)(2,1)S(1)} %shard_map.54.rest_0_), channel_id=1, source_target_pairs={{0,8},{8,0},{16,24},{24,16},{1,9},{9,1},{17,25},{25,17},{2,10},{10... | collective-permute-start | bytes 196616 | tf_op jit(solution)/shard_map/ppermute | solution.py:265
  36.2 4.5 %shard_map.53.left_ref = bf16[2048,64]{1,0:T(8,128)(2,1)S(1)} custom-call(s32[2]{0:T(128)S(1)} %pad_add_fusion.where_ref, bf16[64,1024]{1,0:T(8,128)(2,1)S(1)} %get-tuple-element.20.own_half_ref, bf16[64,1024]{1,0:T(8,128)(2,1)S(1)} %collective-permute-done.4.got_half_ref, bf16[64,128]{1,0:T(8,128)(2,1)S(1)} %get-tuple-element.21.rest_0_, ...), custom_call_target="tpu_custom_call" | custom-call | flops 5000000000 | bytes 589824 | tf_op jit(solution)/shard_map/pallas_call | solution.py:253
  40.8 6.8 %shard_map.55 = (f32[64,1152]{1,0:T(8,128)S(1)}, bf16[64,1152]{1,0:T(8,128)(2,1)S(1)}, f32[64,512]{1,0:T(8,128)S(1)}, bf16[64,512]{1,0:T(8,128)(2,1)S(1)}, bf16[...) custom-call(s32[2]{0:T(128)S(1)} %pad_add_fusion.where_ref, bf16[2048,2048]{1,0:T(8,128)(2,1)S(1)} %bitcast.5, ...), custom_call_target="tpu_custom_call" | custom-call | flops 1610612736 | bytes 8388608 | tf_op jit(solution)/shard_map/pallas_call | solution.py:293
  47.6 1.4 %collective-permute-done.14.got_ref = bf16[64,1152]{1,0:T(8,128)(2,1)S(1)} collective-permute-done((bf16[64,1152]{1,0:T(8,128)(2,1)S(1)}, bf16[64,1152]{1,0:T(8,128)(2,1)S(1)}, u32[]{:S(2)}, u32[]{:S(2)}) %collective-permute-start.14) | collective-permute-done | bytes 147488 | tf_op jit(solution)/shard_map/ppermute | solution.py:265
  49.2 1.7 %collective-permute-start.17 = (bf16[64,1152]{1,0:T(8,128)(2,1)S(1)}, bf16[64,1152]{1,0:T(8,128)(2,1)S(1)}, u32[]{:S(2)}, u32[]{:S(2)}) collective-permute-start(bf16[64,1152]{1,0:T(8,128)(2,1)S(1)} %shard_map.56.refs_0_), channel_id=1, source_target_pairs={{0,6},{1,7},{2,4},{3,5},{4,2},{5,3},{6,0},{7,1},{8,14},{9,15},{10,... | collective-permute-start | bytes 442376 | tf_op jit(solution)/shard_map/ppermute | solution.py:265
  50.8 1.3 %collective-permute-start.16 = (bf16[64,1152]{1,0:T(8,128)(2,1)S(1)}, bf16[64,1152]{1,0:T(8,128)(2,1)S(1)}, u32[]{:S(2)}, u32[]{:S(2)}) collective-permute-start(bf16[64,1152]{1,0:T(8,128)(2,1)S(1)} %shard_map.56.refs_0_), channel_id=1, source_target_pairs={{0,4},{1,5},{2,6},{3,7},{4,0},{5,1},{6,2},{7,3},{8,12},{9,13},{10,... | collective-permute-start | bytes 442376 | tf_op jit(solution)/shard_map/ppermute | solution.py:265
  52.1 0.5 collective-permute-start.15
  52.7 4.2 %collective-permute-done.17.refs_3_ = bf16[64,1152]{1,0:T(8,128)(2,1)S(1)} collective-permute-done((bf16[64,1152]{1,0:T(8,128)(2,1)S(1)}, bf16[64,1152]{1,0:T(8,128)(2,1)S(1)}, u32[]{:S(2)}, u32[]{:S(2)}) %collective-permute-start.17) | collective-permute-done | bytes 147488 | tf_op jit(solution)/shard_map/ppermute | solution.py:265
  56.8 2.3 %collective-permute-done.16.refs_2_ = bf16[64,1152]{1,0:T(8,128)(2,1)S(1)} collective-permute-done((bf16[64,1152]{1,0:T(8,128)(2,1)S(1)}, bf16[64,1152]{1,0:T(8,128)(2,1)S(1)}, u32[]{:S(2)}, u32[]{:S(2)}) %collective-permute-start.16) | collective-permute-done | bytes 147488 | tf_op jit(solution)/shard_map/ppermute | solution.py:265
  59.4 1.2 %collective-permute-start.22 = (bf16[64,512]{1,0:T(8,128)(2,1)S(1)}, bf16[64,512]{1,0:T(8,128)(2,1)S(1)}, u32[]{:S(2)}, u32[]{:S(2)}) collective-permute-start(bf16[64,512]{1,0:T(8,128)(2,1)S(1)} %get-tuple-element.31), channel_id=1, source_target_pairs={{0,8},{8,0},{16,24},{24,16},{1,9},{9,1},{17,25},{25,17},{2,10},{10... | collective-permute-start | bytes 196616 | tf_op jit(solution)/shard_map/ppermute | solution.py:265
  60.6 2.0 %collective-permute-start.23 = (bf16[64,512]{1,0:T(8,128)(2,1)S(1)}, bf16[64,512]{1,0:T(8,128)(2,1)S(1)}, u32[]{:S(2)}, u32[]{:S(2)}) collective-permute-start(bf16[64,512]{1,0:T(8,128)(2,1)S(1)} %get-tuple-element.32), channel_id=1, source_target_pairs={{0,16},{8,24},{16,0},{24,8},{1,17},{9,25},{17,1},{25,9},{2,18},{10... | collective-permute-start | bytes 196616 | tf_op jit(solution)/shard_map/ppermute | solution.py:265
  62.6 1.3 %collective-permute-start.24 = (bf16[64,512]{1,0:T(8,128)(2,1)S(1)}, bf16[64,512]{1,0:T(8,128)(2,1)S(1)}, u32[]{:S(2)}, u32[]{:S(2)}) collective-permute-start(bf16[64,512]{1,0:T(8,128)(2,1)S(1)} %get-tuple-element.33), channel_id=1, source_target_pairs={{0,24},{8,16},{16,8},{24,0},{1,25},{9,17},{17,9},{25,1},{2,26},{10... | collective-permute-start | bytes 196616 | tf_op jit(solution)/shard_map/ppermute | solution.py:265
  63.8 2.6 %collective-permute-start.21 = (bf16[64,128]{1,0:T(8,128)(2,1)S(1)}, bf16[64,128]{1,0:T(8,128)(2,1)S(1)}, u32[]{:S(2)}, u32[]{:S(2)}) collective-permute-start(bf16[64,128]{1,0:T(8,128)(2,1)S(1)} %get-tuple-element.29.rest_0_), channel_id=1, source_target_pairs={{0,24},{8,16},{16,8},{24,0},{1,25},{9,17},{17,9},{25,1},{2,26},{10... | collective-permute-start | bytes 49160 | tf_op jit(solution)/shard_map/ppermute | solution.py:265
  66.6 2.8 %collective-permute-done.23.refs_2_ = bf16[64,512]{1,0:T(8,128)(2,1)S(1)} collective-permute-done((bf16[64,512]{1,0:T(8,128)(2,1)S(1)}, bf16[64,512]{1,0:T(8,128)(2,1)S(1)}, u32[]{:S(2)}, u32[]{:S(2)}) %collective-permute-start.23) | collective-permute-done | bytes 65568 | tf_op jit(solution)/shard_map/ppermute | solution.py:265
  69.5 2.4 %collective-permute-start.27 = (bf16[64,512]{1,0:T(8,128)(2,1)S(1)}, bf16[64,512]{1,0:T(8,128)(2,1)S(1)}, u32[]{:S(2)}, u32[]{:S(2)}) collective-permute-start(bf16[64,512]{1,0:T(8,128)(2,1)S(1)} %shard_map.59.rest_0_), channel_id=1, source_target_pairs={{0,24},{8,16},{16,8},{24,0},{1,25},{9,17},{17,9},{25,1},{2,26},{10... | collective-permute-start | bytes 196616 | tf_op jit(solution)/shard_map/ppermute | solution.py:265
  71.9 1.2 %collective-permute-start.26 = (bf16[64,512]{1,0:T(8,128)(2,1)S(1)}, bf16[64,512]{1,0:T(8,128)(2,1)S(1)}, u32[]{:S(2)}, u32[]{:S(2)}) collective-permute-start(bf16[64,512]{1,0:T(8,128)(2,1)S(1)} %shard_map.59.rest_0_), channel_id=1, source_target_pairs={{0,16},{8,24},{16,0},{24,8},{1,17},{9,25},{17,1},{25,9},{2,18},{10... | collective-permute-start | bytes 196616 | tf_op jit(solution)/shard_map/ppermute | solution.py:265
  73.1 0.9 collective-permute-start.25
  74.0 4.6 %shard_map.58.left_ref = bf16[2048,64]{1,0:T(8,128)(2,1)S(1)} custom-call(s32[2]{0:T(128)S(1)} %pad_add_fusion.where_ref, bf16[64,1024]{1,0:T(8,128)(2,1)S(1)} %get-tuple-element.28.own_half_ref, bf16[64,1024]{1,0:T(8,128)(2,1)S(1)} %collective-permute-done.18.got_half_ref, bf16[64,128]{1,0:T(8,128)(2,1)S(1)} %get-tuple-element.29.rest_0_, ...), custom_call_target="tpu_custom_call" | custom-call | flops 5000000000 | bytes 589824 | tf_op jit(solution)/shard_map/pallas_call | solution.py:253
  78.6 7.0 %shard_map.60 = (bf16[2048,2048]{1,0:T(8,128)(2,1)}, bf16[2048,2048]{1,0:T(8,128)(2,1)}) custom-call(s32[2]{0:T(128)S(1)} %pad_add_fusion.where_ref, bf16[2048,2048]{1,0:T(8,128)(2,1)S(1)} %bitcast.5, bf16[2048,64]{1,0:T(8,128)(2,1)S(1)} %shard_map.58.left_ref, bf16[64,512]{1,0:T(8,128)(2,1)S(1)} %shard_map.59.rest_0_, ...), custom_call_target="tpu_custom_call" | custom-call | flops 536870912 | bytes 8388608 | tf_op jit(solution)/shard_map/pallas_call | solution.py:293
  (45 shorter events, 2.0 us)
Async XLA Ops:
  7.7 1.6 %collective-permute-start = (bf16[64,1152]{1,0:T(8,128)(2,1)S(1)}, bf16[64,1152]{1,0:T(8,128)(2,1)S(1)}, u32[]{:S(2)}, u32[]{:S(2)}) collective-permute-start(bf16[64,1152]{1,0:T(8,128)(2,1)S(1)} %get-tuple-element.19), channel_id=1, source_target_pairs={{0,1},{1,0},{2,3},{3,2},{4,5},{5,4},{6,7},{7,6},{8,9},{9,8},{10,11... | collective-permute-start | bytes 442376 | tf_op jit(solution)/shard_map/ppermute | solution.py:265
  9.4 8.5 %collective-permute-start.3 = (bf16[64,1152]{1,0:T(8,128)(2,1)S(1)}, bf16[64,1152]{1,0:T(8,128)(2,1)S(1)}, u32[]{:S(2)}, u32[]{:S(2)}) collective-permute-start(bf16[64,1152]{1,0:T(8,128)(2,1)S(1)} %shard_map.51.refs_0_), channel_id=1, source_target_pairs={{0,6},{1,7},{2,4},{3,5},{4,2},{5,3},{6,0},{7,1},{8,14},{9,15},{10,... | collective-permute-start | bytes 442376 | tf_op jit(solution)/shard_map/ppermute | solution.py:265
  13.2 7.3 %collective-permute-start.2 = (bf16[64,1152]{1,0:T(8,128)(2,1)S(1)}, bf16[64,1152]{1,0:T(8,128)(2,1)S(1)}, u32[]{:S(2)}, u32[]{:S(2)}) collective-permute-start(bf16[64,1152]{1,0:T(8,128)(2,1)S(1)} %shard_map.51.refs_0_), channel_id=1, source_target_pairs={{0,4},{1,5},{2,6},{3,7},{4,0},{5,1},{6,2},{7,3},{8,12},{9,13},{10,... | collective-permute-start | bytes 442376 | tf_op jit(solution)/shard_map/ppermute | solution.py:265
  13.7 7.1 %collective-permute-start.1 = (bf16[64,1152]{1,0:T(8,128)(2,1)S(1)}, bf16[64,1152]{1,0:T(8,128)(2,1)S(1)}, u32[]{:S(2)}, u32[]{:S(2)}) collective-permute-start(bf16[64,1152]{1,0:T(8,128)(2,1)S(1)} %shard_map.51.refs_0_), channel_id=1, source_target_pairs={{0,2},{1,3},{2,0},{3,1},{4,6},{5,7},{6,4},{7,5},{8,10},{9,11},{10,... | collective-permute-start | bytes 442376 | tf_op jit(solution)/shard_map/ppermute | solution.py:265
  21.1 15.2 %collective-permute-start.4 = (bf16[64,1024]{1,0:T(8,128)(2,1)S(1)}, bf16[64,1024]{1,0:T(8,128)(2,1)S(1)}, u32[]{:S(2)}, u32[]{:S(2)}) collective-permute-start(bf16[64,1024]{1,0:T(8,128)(2,1)S(1)} %get-tuple-element.20.own_half_ref), channel_id=1, source_target_pairs={{0,1},{1,0},{2,3},{3,2},{4,5},{5,4},{6,7},{7,6},{8,9},{9,8},{10,11... | collective-permute-start | bytes 393224 | tf_op jit(solution)/shard_map/ppermute | solution.py:265
  21.1 8.1 %collective-permute-start.8 = (bf16[64,512]{1,0:T(8,128)(2,1)S(1)}, bf16[64,512]{1,0:T(8,128)(2,1)S(1)}, u32[]{:S(2)}, u32[]{:S(2)}) collective-permute-start(bf16[64,512]{1,0:T(8,128)(2,1)S(1)} %get-tuple-element.23), channel_id=1, source_target_pairs={{0,8},{8,0},{16,24},{24,16},{1,9},{9,1},{17,25},{25,17},{2,10},{10... | collective-permute-start | bytes 196616 | tf_op jit(solution)/shard_map/ppermute | solution.py:265
  22.7 8.9 %collective-permute-start.9 = (bf16[64,512]{1,0:T(8,128)(2,1)S(1)}, bf16[64,512]{1,0:T(8,128)(2,1)S(1)}, u32[]{:S(2)}, u32[]{:S(2)}) collective-permute-start(bf16[64,512]{1,0:T(8,128)(2,1)S(1)} %get-tuple-element.24), channel_id=1, source_target_pairs={{0,16},{8,24},{16,0},{24,8},{1,17},{9,25},{17,1},{25,9},{2,18},{10... | collective-permute-start | bytes 196616 | tf_op jit(solution)/shard_map/ppermute | solution.py:265
  25.3 6.4 %collective-permute-start.10 = (bf16[64,512]{1,0:T(8,128)(2,1)S(1)}, bf16[64,512]{1,0:T(8,128)(2,1)S(1)}, u32[]{:S(2)}, u32[]{:S(2)}) collective-permute-start(bf16[64,512]{1,0:T(8,128)(2,1)S(1)} %get-tuple-element.25), channel_id=1, source_target_pairs={{0,24},{8,16},{16,8},{24,0},{1,25},{9,17},{17,9},{25,1},{2,26},{10... | collective-permute-start | bytes 196616 | tf_op jit(solution)/shard_map/ppermute | solution.py:265
  25.5 8.9 %collective-permute-start.7 = (bf16[64,128]{1,0:T(8,128)(2,1)S(1)}, bf16[64,128]{1,0:T(8,128)(2,1)S(1)}, u32[]{:S(2)}, u32[]{:S(2)}) collective-permute-start(bf16[64,128]{1,0:T(8,128)(2,1)S(1)} %get-tuple-element.21.rest_0_), channel_id=1, source_target_pairs={{0,24},{8,16},{16,8},{24,0},{1,25},{9,17},{17,9},{25,1},{2,26},{10... | collective-permute-start | bytes 49160 | tf_op jit(solution)/shard_map/ppermute | solution.py:265
  29.1 6.2 %collective-permute-start.6 = (bf16[64,128]{1,0:T(8,128)(2,1)S(1)}, bf16[64,128]{1,0:T(8,128)(2,1)S(1)}, u32[]{:S(2)}, u32[]{:S(2)}) collective-permute-start(bf16[64,128]{1,0:T(8,128)(2,1)S(1)} %get-tuple-element.21.rest_0_), channel_id=1, source_target_pairs={{0,16},{8,24},{16,0},{24,8},{1,17},{9,25},{17,1},{25,9},{2,18},{10... | collective-permute-start | bytes 49160 | tf_op jit(solution)/shard_map/ppermute | solution.py:265
  31.7 4.6 %collective-permute-start.5 = (bf16[64,128]{1,0:T(8,128)(2,1)S(1)}, bf16[64,128]{1,0:T(8,128)(2,1)S(1)}, u32[]{:S(2)}, u32[]{:S(2)}) collective-permute-start(bf16[64,128]{1,0:T(8,128)(2,1)S(1)} %get-tuple-element.21.rest_0_), channel_id=1, source_target_pairs={{0,8},{8,0},{16,24},{24,16},{1,9},{9,1},{17,25},{25,17},{2,10},{10... | collective-permute-start | bytes 49160 | tf_op jit(solution)/shard_map/ppermute | solution.py:265
  31.7 9.1 %slice-start = ((s8[8388608]{0:T(1024)(128)(4,1)}), s8[4194304]{0:T(1024)(128)(4,1)S(1)}, s32[]{:S(2)}) async-start(s8[8388608]{0:T(1024)(128)(4,1)} %bitcast.4), calls=%async_computation | async-start | bytes 8388608
  31.7 9.0 %slice-start.1 = ((s8[8388608]{0:T(1024)(128)(4,1)}), s8[4194304]{0:T(1024)(128)(4,1)S(1)}, s32[]{:S(2)}) async-start(s8[8388608]{0:T(1024)(128)(4,1)} %bitcast.4), calls=%async_computation.1 | async-start | bytes 8388608
  31.7 9.0 %copy-start = (bf16[2048,64]{0,1:T(8,128)(2,1)S(1)}, bf16[2048,64]{0,1:T(8,128)(2,1)}, u32[]{:S(2)}) copy-start(bf16[2048,64]{0,1:T(8,128)(2,1)} %param.4) | copy-start | bytes 786436
  31.7 9.0 %copy-start.1 = (bf16[2048,64]{0,1:T(8,128)(2,1)S(1)}, bf16[2048,64]{0,1:T(8,128)(2,1)}, u32[]{:S(2)}) copy-start(bf16[2048,64]{0,1:T(8,128)(2,1)} %param.5) | copy-start | bytes 786436
  31.8 8.9 %collective-permute-start.13 = (bf16[64,512]{1,0:T(8,128)(2,1)S(1)}, bf16[64,512]{1,0:T(8,128)(2,1)S(1)}, u32[]{:S(2)}, u32[]{:S(2)}) collective-permute-start(bf16[64,512]{1,0:T(8,128)(2,1)S(1)} %shard_map.54.rest_0_), channel_id=1, source_target_pairs={{0,24},{8,16},{16,8},{24,0},{1,25},{9,17},{17,9},{25,1},{2,26},{10... | collective-permute-start | bytes 196616 | tf_op jit(solution)/shard_map/ppermute | solution.py:265
  34.4 6.3 %collective-permute-start.12 = (bf16[64,512]{1,0:T(8,128)(2,1)S(1)}, bf16[64,512]{1,0:T(8,128)(2,1)S(1)}, u32[]{:S(2)}, u32[]{:S(2)}) collective-permute-start(bf16[64,512]{1,0:T(8,128)(2,1)S(1)} %shard_map.54.rest_0_), channel_id=1, source_target_pairs={{0,16},{8,24},{16,0},{24,8},{1,17},{9,25},{17,1},{25,9},{2,18},{10... | collective-permute-start | bytes 196616 | tf_op jit(solution)/shard_map/ppermute | solution.py:265
  35.3 5.4 %collective-permute-start.11 = (bf16[64,512]{1,0:T(8,128)(2,1)S(1)}, bf16[64,512]{1,0:T(8,128)(2,1)S(1)}, u32[]{:S(2)}, u32[]{:S(2)}) collective-permute-start(bf16[64,512]{1,0:T(8,128)(2,1)S(1)} %shard_map.54.rest_0_), channel_id=1, source_target_pairs={{0,8},{8,0},{16,24},{24,16},{1,9},{9,1},{17,25},{25,17},{2,10},{10... | collective-permute-start | bytes 196616 | tf_op jit(solution)/shard_map/ppermute | solution.py:265
  47.6 1.4 %collective-permute-start.14 = (bf16[64,1152]{1,0:T(8,128)(2,1)S(1)}, bf16[64,1152]{1,0:T(8,128)(2,1)S(1)}, u32[]{:S(2)}, u32[]{:S(2)}) collective-permute-start(bf16[64,1152]{1,0:T(8,128)(2,1)S(1)} %get-tuple-element.27), channel_id=1, source_target_pairs={{0,1},{1,0},{2,3},{3,2},{4,5},{5,4},{6,7},{7,6},{8,9},{9,8},{10,11... | collective-permute-start | bytes 442376 | tf_op jit(solution)/shard_map/ppermute | solution.py:265
  49.2 7.7 %collective-permute-start.17 = (bf16[64,1152]{1,0:T(8,128)(2,1)S(1)}, bf16[64,1152]{1,0:T(8,128)(2,1)S(1)}, u32[]{:S(2)}, u32[]{:S(2)}) collective-permute-start(bf16[64,1152]{1,0:T(8,128)(2,1)S(1)} %shard_map.56.refs_0_), channel_id=1, source_target_pairs={{0,6},{1,7},{2,4},{3,5},{4,2},{5,3},{6,0},{7,1},{8,14},{9,15},{10,... | collective-permute-start | bytes 442376 | tf_op jit(solution)/shard_map/ppermute | solution.py:265
  50.8 8.3 %collective-permute-start.16 = (bf16[64,1152]{1,0:T(8,128)(2,1)S(1)}, bf16[64,1152]{1,0:T(8,128)(2,1)S(1)}, u32[]{:S(2)}, u32[]{:S(2)}) collective-permute-start(bf16[64,1152]{1,0:T(8,128)(2,1)S(1)} %shard_map.56.refs_0_), channel_id=1, source_target_pairs={{0,4},{1,5},{2,6},{3,7},{4,0},{5,1},{6,2},{7,3},{8,12},{9,13},{10,... | collective-permute-start | bytes 442376 | tf_op jit(solution)/shard_map/ppermute | solution.py:265
  52.1 7.0 %collective-permute-start.15 = (bf16[64,1152]{1,0:T(8,128)(2,1)S(1)}, bf16[64,1152]{1,0:T(8,128)(2,1)S(1)}, u32[]{:S(2)}, u32[]{:S(2)}) collective-permute-start(bf16[64,1152]{1,0:T(8,128)(2,1)S(1)} %shard_map.56.refs_0_), channel_id=1, source_target_pairs={{0,2},{1,3},{2,0},{3,1},{4,6},{5,7},{6,4},{7,5},{8,10},{9,11},{10,... | collective-permute-start | bytes 442376 | tf_op jit(solution)/shard_map/ppermute | solution.py:265
  59.4 14.6 %collective-permute-start.18 = (bf16[64,1024]{1,0:T(8,128)(2,1)S(1)}, bf16[64,1024]{1,0:T(8,128)(2,1)S(1)}, u32[]{:S(2)}, u32[]{:S(2)}) collective-permute-start(bf16[64,1024]{1,0:T(8,128)(2,1)S(1)} %get-tuple-element.28.own_half_ref), channel_id=1, source_target_pairs={{0,1},{1,0},{2,3},{3,2},{4,5},{5,4},{6,7},{7,6},{8,9},{9,8},{10,11... | collective-permute-start | bytes 393224 | tf_op jit(solution)/shard_map/ppermute | solution.py:265
  59.4 7.0 %collective-permute-start.22 = (bf16[64,512]{1,0:T(8,128)(2,1)S(1)}, bf16[64,512]{1,0:T(8,128)(2,1)S(1)}, u32[]{:S(2)}, u32[]{:S(2)}) collective-permute-start(bf16[64,512]{1,0:T(8,128)(2,1)S(1)} %get-tuple-element.31), channel_id=1, source_target_pairs={{0,8},{8,0},{16,24},{24,16},{1,9},{9,1},{17,25},{25,17},{2,10},{10... | collective-permute-start | bytes 196616 | tf_op jit(solution)/shard_map/ppermute | solution.py:265
  60.6 8.9 %collective-permute-start.23 = (bf16[64,512]{1,0:T(8,128)(2,1)S(1)}, bf16[64,512]{1,0:T(8,128)(2,1)S(1)}, u32[]{:S(2)}, u32[]{:S(2)}) collective-permute-start(bf16[64,512]{1,0:T(8,128)(2,1)S(1)} %get-tuple-element.32), channel_id=1, source_target_pairs={{0,16},{8,24},{16,0},{24,8},{1,17},{9,25},{17,1},{25,9},{2,18},{10... | collective-permute-start | bytes 196616 | tf_op jit(solution)/shard_map/ppermute | solution.py:265
  62.6 6.9 %collective-permute-start.24 = (bf16[64,512]{1,0:T(8,128)(2,1)S(1)}, bf16[64,512]{1,0:T(8,128)(2,1)S(1)}, u32[]{:S(2)}, u32[]{:S(2)}) collective-permute-start(bf16[64,512]{1,0:T(8,128)(2,1)S(1)} %get-tuple-element.33), channel_id=1, source_target_pairs={{0,24},{8,16},{16,8},{24,0},{1,25},{9,17},{17,9},{25,1},{2,26},{10... | collective-permute-start | bytes 196616 | tf_op jit(solution)/shard_map/ppermute | solution.py:265
  63.8 8.1 %collective-permute-start.21 = (bf16[64,128]{1,0:T(8,128)(2,1)S(1)}, bf16[64,128]{1,0:T(8,128)(2,1)S(1)}, u32[]{:S(2)}, u32[]{:S(2)}) collective-permute-start(bf16[64,128]{1,0:T(8,128)(2,1)S(1)} %get-tuple-element.29.rest_0_), channel_id=1, source_target_pairs={{0,24},{8,16},{16,8},{24,0},{1,25},{9,17},{17,9},{25,1},{2,26},{10... | collective-permute-start | bytes 49160 | tf_op jit(solution)/shard_map/ppermute | solution.py:265
  66.4 6.7 %collective-permute-start.20 = (bf16[64,128]{1,0:T(8,128)(2,1)S(1)}, bf16[64,128]{1,0:T(8,128)(2,1)S(1)}, u32[]{:S(2)}, u32[]{:S(2)}) collective-permute-start(bf16[64,128]{1,0:T(8,128)(2,1)S(1)} %get-tuple-element.29.rest_0_), channel_id=1, source_target_pairs={{0,16},{8,24},{16,0},{24,8},{1,17},{9,25},{17,1},{25,9},{2,18},{10... | collective-permute-start | bytes 49160 | tf_op jit(solution)/shard_map/ppermute | solution.py:265
  69.5 4.5 %collective-permute-start.19 = (bf16[64,128]{1,0:T(8,128)(2,1)S(1)}, bf16[64,128]{1,0:T(8,128)(2,1)S(1)}, u32[]{:S(2)}, u32[]{:S(2)}) collective-permute-start(bf16[64,128]{1,0:T(8,128)(2,1)S(1)} %get-tuple-element.29.rest_0_), channel_id=1, source_target_pairs={{0,8},{8,0},{16,24},{24,16},{1,9},{9,1},{17,25},{25,17},{2,10},{10... | collective-permute-start | bytes 49160 | tf_op jit(solution)/shard_map/ppermute | solution.py:265
  69.5 9.1 %collective-permute-start.27 = (bf16[64,512]{1,0:T(8,128)(2,1)S(1)}, bf16[64,512]{1,0:T(8,128)(2,1)S(1)}, u32[]{:S(2)}, u32[]{:S(2)}) collective-permute-start(bf16[64,512]{1,0:T(8,128)(2,1)S(1)} %shard_map.59.rest_0_), channel_id=1, source_target_pairs={{0,24},{8,16},{16,8},{24,0},{1,25},{9,17},{17,9},{25,1},{2,26},{10... | collective-permute-start | bytes 196616 | tf_op jit(solution)/shard_map/ppermute | solution.py:265
  71.9 6.7 %collective-permute-start.26 = (bf16[64,512]{1,0:T(8,128)(2,1)S(1)}, bf16[64,512]{1,0:T(8,128)(2,1)S(1)}, u32[]{:S(2)}, u32[]{:S(2)}) collective-permute-start(bf16[64,512]{1,0:T(8,128)(2,1)S(1)} %shard_map.59.rest_0_), channel_id=1, source_target_pairs={{0,16},{8,24},{16,0},{24,8},{1,17},{9,25},{17,1},{25,9},{2,18},{10... | collective-permute-start | bytes 196616 | tf_op jit(solution)/shard_map/ppermute | solution.py:265
  73.1 5.5 %collective-permute-start.25 = (bf16[64,512]{1,0:T(8,128)(2,1)S(1)}, bf16[64,512]{1,0:T(8,128)(2,1)S(1)}, u32[]{:S(2)}, u32[]{:S(2)}) collective-permute-start(bf16[64,512]{1,0:T(8,128)(2,1)S(1)} %shard_map.59.rest_0_), channel_id=1, source_target_pairs={{0,8},{8,0},{16,24},{24,16},{1,9},{9,1},{17,25},{25,17},{2,10},{10... | collective-permute-start | bytes 196616 | tf_op jit(solution)/shard_map/ppermute | solution.py:265
